TPU v7x, 32 devices: a whole 2x2x4 slice. The times are simulated.
32 devices in a mesh: dp: 16 (over z, y, x), mp: 2 (over core).
Axes of the slice: x: 2, y: 2, z: 4, core: 2. Of those that a mesh axis runs over, the one named last changes fastest.
Arguments:
- tokens: bfloat16 [32768, 768], P('dp'), may hold values from -6 to 6
- cond: bfloat16 [32768, 128], P('dp'), may hold values from -6 to 6
- segments: int32 [32, 1024], P('dp'), may hold values from 0 to 3, never falling along the last dimension, each value on 1 to 512 neighbouring positions
- out_grad: bfloat16 [32768, 768], P('dp'), may hold values from -6 to 6
- step: int32 [1], replicated, may hold values from 2 to 20
- ada_weight: float32 [128, 4608], P(None, 'dp'), may hold values from -0.5 to 0.5
- ada_first: float32 [128, 4608], P(None, 'dp'), may hold values from -0.00061035156 to 0.00061035156
- ada_second: float32 [128, 4608], P(None, 'dp'), may hold values from 1.3031258e-10 to 5.212503e-10
- norm_params: float32 [8, 768], P(None, 'dp'), may hold values from 0.5 to 1.5
- norm_first: float32 [8, 768], P(None, 'dp'), may hold values from -0.0024414062 to 0.0024414062
- norm_second: float32 [8, 768], P(None, 'dp'), may hold values from 2.6062516e-10 to 1.0425006e-09
- qkv_weight: float32 [3, 768, 768], P(None, 'dp', 'mp'), may hold values from -0.109375 to 0.109375
- qkv_first: float32 [3, 768, 768], P(None, 'dp', 'mp'), may hold values from -0.00061035156 to 0.00061035156
- qkv_second: float32 [3, 768, 768], P(None, 'dp', 'mp'), may hold values from 1.3031258e-10 to 5.212503e-10
- out_weight: float32 [768, 768], P('mp', 'dp'), may hold values from -1.75 to 1.75
- out_first: float32 [768, 768], P('mp', 'dp'), may hold values from -0.00061035156 to 0.00061035156
- out_second: float32 [768, 768], P('mp', 'dp'), may hold values from 1.6289073e-11 to 6.515629e-11
- up_weight: float32 [768, 3072], P('dp', 'mp'), may hold values from -0.21875 to 0.21875
- up_first: float32 [768, 3072], P('dp', 'mp'), may hold values from -0.00061035156 to 0.00061035156
- up_second: float32 [768, 3072], P('dp', 'mp'), may hold values from 1.3031258e-10 to 5.212503e-10
- down_weight: float32 [3072, 768], P('mp', 'dp'), may hold values from -0.109375 to 0.109375
- down_first: float32 [3072, 768], P('mp', 'dp'), may hold values from -0.00061035156 to 0.00061035156
- down_second: float32 [3072, 768], P('mp', 'dp'), may hold values from 1.3031258e-10 to 5.212503e-10
Outputs:
- result: bfloat16 [32768, 768], P('dp')
- input_grad: float32 [32768, 768], P('dp')
- grad_norm: float32 [1], replicated
- ada_weight_next: float32 [128, 4608], P(None, 'dp')
- ada_first_next: float32 [128, 4608], P(None, 'dp')
- ada_second_next: float32 [128, 4608], P(None, 'dp')
- norm_params_next: float32 [8, 768], P(None, 'dp')
- norm_first_next: float32 [8, 768], P(None, 'dp')
- norm_second_next: float32 [8, 768], P(None, 'dp')
- qkv_weight_next: float32 [3, 768, 768], P(None, 'dp', 'mp')
- qkv_first_next: float32 [3, 768, 768], P(None, 'dp', 'mp')
- qkv_second_next: float32 [3, 768, 768], P(None, 'dp', 'mp')
- out_weight_next: float32 [768, 768], P('mp', 'dp')
- out_first_next: float32 [768, 768], P('mp', 'dp')
- out_second_next: float32 [768, 768], P('mp', 'dp')
- up_weight_next: float32 [768, 3072], P('dp', 'mp')
- up_first_next: float32 [768, 3072], P('dp', 'mp')
- up_second_next: float32 [768, 3072], P('dp', 'mp')
- down_weight_next: float32 [3072, 768], P('mp', 'dp')
- down_first_next: float32 [3072, 768], P('mp', 'dp')
- down_second_next: float32 [3072, 768], P('mp', 'dp')
Inputs may be any that keep to these rules, and one draw needn't show every extreme that they name: `segments`: along each sequence document ids never fall; each document holds 1 to 512 positions, and one document of a sequence holds exactly 512.
All inputs are finite; a program needn't handle non-finite values.
Results may differ from a plain program's by a relative error of at most 0.012.
The roundings to bfloat16 on the way count: a program that leaves them out, or rounds other values in their place, can miss the bound.
Values may be sent and summed in bfloat16 or wider, within the bound.
A program may use at most 320 MiB of HBM per device.

v0:
```python
import math

import jax
import jax.numpy as jnp
from jax import lax
from jax.sharding import PartitionSpec as P

HEAD_DIM = 64


clip_limit = 1.0
step_rates = (0.075, 0.75, 0.075, 0.25, 0.075, 0.075)
decay_rates = (0.01, 0.0, 0.01, 0.01, 0.01, 0.01)


def modnorm(inputs, gain_row, shift_row, scale_row):
    centre = inputs - jnp.mean(inputs, axis=-1, keepdims=True)
    spread = jnp.mean(centre * centre, axis=-1, keepdims=True)
    return centre * lax.rsqrt(spread + 1e-05) * gain_row * (1.0 + scale_row) + shift_row


def rope_tables(length, head_size):
    half_dim = head_size // 2
    inverse = jnp.exp(
        jnp.arange(half_dim, dtype=jnp.float32) * (-2.0 * math.log(10000.0) / head_size)
    )
    angles = jnp.arange(length, dtype=jnp.float32)[:, None] * inverse[None, :]
    return (jnp.cos(angles), jnp.sin(angles))


def rotate(values, cosines, sines):
    half_dim = values.shape[-1] // 2
    first_half = values[..., :half_dim]
    second_half = values[..., half_dim:]
    cos_row = cosines[:, None, :]
    sin_row = sines[:, None, :]
    return jnp.concatenate(
        [
            first_half * cos_row - second_half * sin_row,
            second_half * cos_row + first_half * sin_row,
        ],
        axis=-1,
    )


def unrotate(grads, cosines, sines):
    half_dim = grads.shape[-1] // 2
    first_half = grads[..., :half_dim]
    second_half = grads[..., half_dim:]
    cos_row = cosines[:, None, :]
    sin_row = sines[:, None, :]
    return jnp.concatenate(
        [
            first_half * cos_row + second_half * sin_row,
            second_half * cos_row - first_half * sin_row,
        ],
        axis=-1,
    )


def gelu_tanh(values):
    return jax.nn.gelu(values, approximate=True)


def adam_update(
    weight, first_moment, second_moment, grad_mean, clip_factor, step_count, step_rate, decay_rate
):
    clipped = grad_mean * clip_factor
    first_new = 0.9 * first_moment + 0.1 * clipped
    second_new = 0.999 * second_moment + 0.001 * clipped * clipped
    fix_one = 1.0 - jnp.exp(step_count * math.log(0.9))
    fix_two = 1.0 - jnp.exp(step_count * math.log(0.999))
    update = first_new / fix_one / (jnp.sqrt(second_new / fix_two) + 1e-08) + decay_rate * weight
    return (weight - step_rate * update, first_new, second_new)


def per_device(
    tokens,
    cond,
    segments,
    out_grad,
    step,
    ada_weight,
    ada_first,
    ada_second,
    norm_params,
    norm_first,
    norm_second,
    qkv_weight,
    qkv_first,
    qkv_second,
    out_weight,
    out_first,
    out_second,
    up_weight,
    up_first,
    up_second,
    down_weight,
    down_first,
    down_second,
):
    ada_low, norm_low, qkv_low, out_low, up_low, down_low = (
        lax.all_gather(ada_weight.astype(jnp.bfloat16), "dp", axis=1, tiled=True),
        lax.all_gather(norm_params.astype(jnp.bfloat16), "dp", axis=1, tiled=True),
        lax.all_gather(qkv_weight.astype(jnp.bfloat16), "dp", axis=1, tiled=True),
        lax.all_gather(out_weight.astype(jnp.bfloat16), "dp", axis=1, tiled=True),
        lax.all_gather(up_weight.astype(jnp.bfloat16), "dp", axis=0, tiled=True),
        lax.all_gather(down_weight.astype(jnp.bfloat16), "dp", axis=1, tiled=True),
    )
    model_width = norm_low.shape[1]
    tok_rows = tokens.shape[0]
    seq_count = segments.shape[0]
    seq_length = segments.shape[1]
    heads_local = qkv_low.shape[2] // HEAD_DIM
    score_scale = HEAD_DIM ** (-0.5)
    cosines, sines = rope_tables(seq_length, HEAD_DIM)
    inputs = tokens.astype(jnp.float32)
    cond_low = jax.nn.silu(cond.astype(jnp.float32)).astype(jnp.bfloat16)
    norm_vals = norm_low.astype(jnp.float32)
    modulation = jnp.dot(cond_low, ada_low, preferred_element_type=jnp.float32) + norm_vals[
        2:
    ].reshape(-1)
    shift_one = modulation[:, 0:model_width]
    scale_one = modulation[:, model_width : 2 * model_width]
    gate_one = modulation[:, 2 * model_width : 3 * model_width]
    shift_two = modulation[:, 3 * model_width : 4 * model_width]
    scale_two = modulation[:, 4 * model_width : 5 * model_width]
    gate_two = modulation[:, 5 * model_width : 6 * model_width]
    h_one = modnorm(inputs, norm_vals[0], shift_one, scale_one).astype(jnp.bfloat16)
    projected = jnp.einsum("td,cde->cte", h_one, qkv_low, preferred_element_type=jnp.float32)
    shaped = projected.reshape(3, seq_count, seq_length, heads_local, HEAD_DIM)
    queries = rotate(shaped[0], cosines, sines).astype(jnp.bfloat16)
    keys = rotate(shaped[1], cosines, sines).astype(jnp.bfloat16)
    values = shaped[2].astype(jnp.bfloat16)

    def scores_of(query_block, key_block, segment_row):
        raw_scores = jnp.einsum(
            "qhd,khd->hqk", query_block, key_block, preferred_element_type=jnp.float32
        )
        same_doc = segment_row[:, None] == segment_row[None, :]
        return jnp.where(same_doc[None], raw_scores * score_scale, -1e30)

    def attend(packed):
        query_block, key_block, value_block, segment_row = packed
        scores = scores_of(query_block, key_block, segment_row)
        row_top = jnp.max(scores, axis=-1, keepdims=True)
        row_total = jnp.sum(jnp.exp(scores - row_top), axis=-1, keepdims=True)
        logsum = row_top + jnp.log(row_total)
        softmax_w = jnp.exp(scores - logsum).astype(jnp.bfloat16)
        mixed_out = jnp.einsum(
            "hqk,khd->qhd", softmax_w, value_block, preferred_element_type=jnp.float32
        )
        return (mixed_out.astype(jnp.bfloat16), logsum)

    attended, logsums = lax.map(attend, (queries, keys, values, segments))
    attn_flat = attended.reshape(tok_rows, -1)
    attn_part = jnp.dot(attn_flat, out_low, preferred_element_type=jnp.float32)
    branch = lax.psum(attn_part, "mp")
    middle = inputs + gate_one * branch
    h_two = modnorm(middle, norm_vals[1], shift_two, scale_two).astype(jnp.bfloat16)
    hidden_pre = jnp.dot(h_two, up_low, preferred_element_type=jnp.float32)
    hidden = gelu_tanh(hidden_pre).astype(jnp.bfloat16)
    mlp_part = jnp.dot(hidden, down_low, preferred_element_type=jnp.float32)
    cotangent = out_grad.astype(jnp.float32)
    mlp_out = lax.psum(mlp_part, "mp")
    result = (middle + gate_two * mlp_out).astype(jnp.bfloat16)
    d_gate_two = cotangent * mlp_out
    mlp_grad = (gate_two * cotangent).astype(jnp.bfloat16)
    grad_down = jnp.einsum("tf,td->fd", hidden, mlp_grad, preferred_element_type=jnp.float32)
    grad_hidden = jnp.einsum("td,fd->tf", mlp_grad, down_low, preferred_element_type=jnp.float32)
    unused_gelu, gelu_back = jax.vjp(gelu_tanh, hidden_pre)
    grad_pre = gelu_back(grad_hidden)[0].astype(jnp.bfloat16)
    grad_up = jnp.einsum("td,tf->df", h_two, grad_pre, preferred_element_type=jnp.float32)
    h_two_part = jnp.einsum("tf,df->td", grad_pre, up_low, preferred_element_type=jnp.float32)
    h_two_grad = lax.psum(h_two_part, "mp")
    unused_two, norm_two_back = jax.vjp(modnorm, middle, norm_vals[1], shift_two, scale_two)
    d_middle, d_gain_two, d_shift_two, d_scale_two = norm_two_back(h_two_grad)
    middle_grad = cotangent + d_middle
    attn_grad = (gate_one * middle_grad).astype(jnp.bfloat16)
    d_gate_one = middle_grad * branch
    grad_out = jnp.einsum("te,td->ed", attn_flat, attn_grad, preferred_element_type=jnp.float32)
    out_back = jnp.einsum(
        "td,ed->te", attn_grad, out_low, preferred_element_type=jnp.float32
    ).astype(jnp.bfloat16)
    grad_attended = out_back.reshape(seq_count, seq_length, heads_local, HEAD_DIM)

    def attend_back(packed):
        query_block, key_block, value_block, segment_row, logsum, upstream = packed
        scores = scores_of(query_block, key_block, segment_row)
        softmax_w = jnp.exp(scores - logsum)
        grad_weights = jnp.einsum(
            "qhd,khd->hqk", upstream, value_block, preferred_element_type=jnp.float32
        )
        grad_value = jnp.einsum(
            "hqk,qhd->khd",
            softmax_w.astype(jnp.bfloat16),
            upstream,
            preferred_element_type=jnp.float32,
        )
        row_delta = jnp.sum(softmax_w * grad_weights, axis=-1, keepdims=True)
        grad_scores = (softmax_w * (grad_weights - row_delta) * score_scale).astype(jnp.bfloat16)
        grad_query = jnp.einsum(
            "hqk,khd->qhd", grad_scores, key_block, preferred_element_type=jnp.float32
        )
        grad_key = jnp.einsum(
            "hqk,qhd->khd", grad_scores, query_block, preferred_element_type=jnp.float32
        )
        return (grad_query, grad_key, grad_value)

    grad_q, grad_k, grad_v = lax.map(
        attend_back, (queries, keys, values, segments, logsums, grad_attended)
    )
    grad_proj = (
        jnp.stack([unrotate(grad_q, cosines, sines), unrotate(grad_k, cosines, sines), grad_v])
        .reshape(3, tok_rows, -1)
        .astype(jnp.bfloat16)
    )
    grad_qkv = jnp.einsum("td,cte->cde", h_one, grad_proj, preferred_element_type=jnp.float32)
    h_one_part = jnp.einsum("cte,cde->td", grad_proj, qkv_low, preferred_element_type=jnp.float32)
    h_one_grad = lax.psum(h_one_part, "mp")
    unused_one, norm_one_back = jax.vjp(modnorm, inputs, norm_vals[0], shift_one, scale_one)
    d_inputs, d_gain_one, d_shift_one, d_scale_one = norm_one_back(h_one_grad)
    input_grad = middle_grad + d_inputs
    grad_mod = jnp.concatenate(
        [d_shift_one, d_scale_one, d_gate_one, d_shift_two, d_scale_two, d_gate_two], axis=1
    ).astype(jnp.bfloat16)
    grad_ada = jnp.einsum("tc,tm->cm", cond_low, grad_mod, preferred_element_type=jnp.float32)
    bias_grad = jnp.sum(grad_mod.astype(jnp.float32), axis=0).reshape(6, model_width)
    grad_norm_rows = jnp.concatenate([d_gain_one[None], d_gain_two[None], bias_grad], axis=0)
    ada_sum, norm_sum, qkv_sum, out_sum, up_sum, down_sum = (
        lax.psum_scatter(grad_ada, "dp", scatter_dimension=1, tiled=True),
        lax.psum_scatter(grad_norm_rows, "dp", scatter_dimension=1, tiled=True),
        lax.psum_scatter(grad_qkv, "dp", scatter_dimension=1, tiled=True),
        lax.psum_scatter(grad_out, "dp", scatter_dimension=1, tiled=True),
        lax.psum_scatter(grad_up, "dp", scatter_dimension=0, tiled=True),
        lax.psum_scatter(grad_down, "dp", scatter_dimension=1, tiled=True),
    )
    token_total = float(tok_rows * lax.axis_size("dp"))
    ada_mean = ada_sum / token_total
    norm_mean = norm_sum / token_total
    qkv_mean = qkv_sum / token_total
    out_mean = out_sum / token_total
    up_mean = up_sum / token_total
    down_mean = down_sum / token_total
    shared_part = 1.0 / lax.axis_size("mp")
    local_sq = (
        jnp.sum(qkv_mean * qkv_mean)
        + jnp.sum(out_mean * out_mean)
        + jnp.sum(up_mean * up_mean)
        + jnp.sum(down_mean * down_mean)
        + shared_part * (jnp.sum(ada_mean * ada_mean) + jnp.sum(norm_mean * norm_mean))
    )
    total_sq = lax.psum(local_sq, ("dp", "mp"))
    grad_norm = jnp.sqrt(total_sq)
    clip_factor = jnp.minimum(1.0, clip_limit / (grad_norm + 1e-06))
    step_count = step[0].astype(jnp.float32)
    ada_new = adam_update(
        ada_weight,
        ada_first,
        ada_second,
        ada_mean,
        clip_factor,
        step_count,
        step_rates[0],
        decay_rates[0],
    )
    norm_new = adam_update(
        norm_params,
        norm_first,
        norm_second,
        norm_mean,
        clip_factor,
        step_count,
        step_rates[1],
        decay_rates[1],
    )
    qkv_new = adam_update(
        qkv_weight,
        qkv_first,
        qkv_second,
        qkv_mean,
        clip_factor,
        step_count,
        step_rates[2],
        decay_rates[2],
    )
    out_new = adam_update(
        out_weight,
        out_first,
        out_second,
        out_mean,
        clip_factor,
        step_count,
        step_rates[3],
        decay_rates[3],
    )
    up_new = adam_update(
        up_weight,
        up_first,
        up_second,
        up_mean,
        clip_factor,
        step_count,
        step_rates[4],
        decay_rates[4],
    )
    down_new = adam_update(
        down_weight,
        down_first,
        down_second,
        down_mean,
        clip_factor,
        step_count,
        step_rates[5],
        decay_rates[5],
    )
    return (
        result,
        input_grad,
        grad_norm.reshape(1),
        ada_new[0],
        ada_new[1],
        ada_new[2],
        norm_new[0],
        norm_new[1],
        norm_new[2],
        qkv_new[0],
        qkv_new[1],
        qkv_new[2],
        out_new[0],
        out_new[1],
        out_new[2],
        up_new[0],
        up_new[1],
        up_new[2],
        down_new[0],
        down_new[1],
        down_new[2],
    )


def solution(mesh):
    return jax.shard_map(
        per_device,
        mesh=mesh,
        in_specs=(
            P("dp", None),
            P("dp", None),
            P("dp", None),
            P("dp", None),
            P(),
            P(None, "dp"),
            P(None, "dp"),
            P(None, "dp"),
            P(None, "dp"),
            P(None, "dp"),
            P(None, "dp"),
            P(None, "dp", "mp"),
            P(None, "dp", "mp"),
            P(None, "dp", "mp"),
            P("mp", "dp"),
            P("mp", "dp"),
            P("mp", "dp"),
            P("dp", "mp"),
            P("dp", "mp"),
            P("dp", "mp"),
            P("mp", "dp"),
            P("mp", "dp"),
            P("mp", "dp"),
        ),
        out_specs=(
            P("dp", None),
            P("dp", None),
            P(),
            P(None, "dp"),
            P(None, "dp"),
            P(None, "dp"),
            P(None, "dp"),
            P(None, "dp"),
            P(None, "dp"),
            P(None, "dp", "mp"),
            P(None, "dp", "mp"),
            P(None, "dp", "mp"),
            P("mp", "dp"),
            P("mp", "dp"),
            P("mp", "dp"),
            P("dp", "mp"),
            P("dp", "mp"),
            P("dp", "mp"),
            P("mp", "dp"),
            P("mp", "dp"),
            P("mp", "dp"),
        ),
        check_vma=False,
    )
```

profile of v0, /device:TPU:0, one launch (start us, length us, event | category | flops | bytes accessed | tf_op | source)
XLA Modules:
  0.0 1853.0 jit_solution(10040764894950794897)
XLA Ops:
  16.6 42.8 %all-gather = bf16[16,48,8]{1,2,0:T(8,128)(2,1)S(1)} all-gather(bf16[1,48,8]{1,2,0:T(8,128)(2,1)S(1)} %convert_bitcast_fusion), channel_id=1, replica_groups=mesh['dp'=16,'mp'=2] {'dp'}, dimensions={0}, use_global_device_ids=true | all-gather | bytes 13056 | tf_op jit(solution)/shard_map/all_gather | solution.py:104
  60.7 43.1 %all_gather.21 = bf16[384,768]{0,1:T(8,128)(2,1)} all-gather(bf16[384,48]{0,1:T(8,128)(2,1)S(1)} %convert_element_type.96), channel_id=1, replica_groups=mesh['dp'=16,'mp'=2] {'dp'}, dimensions={1}, use_global_device_ids=true | all-gather | bytes 626688 | tf_op jit(solution)/shard_map/all_gather | solution.py:106
  103.8 16.4 convolution_add_fusion
  174.8 70.6 %while.26 = (s32[]{:T(128)}, bf16[2,1024,6,64]{1,3,2,0:T(8,128)(2,1)S(1)}, f32[2,6,1024,1]{2,1,3,0:T(8,128)S(1)}, bf16[2,1024,6,64]{1,3,2,0:T(8,128)(2,1)}, s32[...) while((s32[]{:T(128)}, ...), condition=%wide.region_5.6_spmd, body=%wide.region_2.5_spmd.sunk | while | flops 1681254400 | bytes 83089512 | solution.py:155
  255.9 28.3 %all-reduce.7.cloned.1.call-done = f32[2048,768]{1,0:T(8,128)} async-done(((f32[2048,768]{1,0:T(8,128)}), f32[2048,768]{1,0:T(8,128)}) %all-reduce.7.cloned.1.call-update) | async-done | bytes 6291472 | tf_op jit(solution)/shard_map/psum | solution.py:158
  299.2 52.1 %all-gather.10.cloned.1.call-done = bf16[768,1536]{1,0:T(8,128)(2,1)} async-done(((bf16[48,1536]{1,0:T(8,128)(2,1)}), bf16[768,1536]{1,0:T(8,128)(2,1)}) %all-gather.10.cloned.1.call-update) | async-done | bytes 2359312 | tf_op jit(solution)/shard_map/all_gather | solution.py:107
  364.3 51.7 %all-gather.12.cloned.1.call-done = bf16[1536,768]{0,1:T(8,128)(2,1)} async-done(((bf16[1536,48]{0,1:T(8,128)(2,1)}), bf16[1536,768]{0,1:T(8,128)(2,1)}) %all-gather.12.cloned.1.call-update) | async-done | bytes 2359312 | tf_op jit(solution)/shard_map/all_gather | solution.py:108
  451.9 20.8 %all-reduce.9.cloned.1.call-done = f32[2048,768]{1,0:T(8,128)} async-done(((f32[2048,768]{1,0:T(8,128)}), f32[2048,768]{1,0:T(8,128)}) %all-reduce.9.cloned.1.call-update) | async-done | bytes 6291472 | tf_op jit(solution)/shard_map/psum | solution.py:175
  500.0 338.8 %while.27 = (s32[]{:T(128)}, f32[2,1024,6,64]{1,0,3,2:T(2,128)}, f32[2,1024,6,64]{1,0,3,2:T(2,128)}, bf16[2,1024,6,64]{1,3,2,0:T(8,128)(2,1)}, bf16[2,1024,6,64]...) while((s32[]{:T(128)}, f32[2,1024,6,64]{1,0,3,2:T(2,128)}, ...), condition=%wide.region_15.16_spmd, body=%wide.region_13.15_spmd.sunk | while | flops 4191172608 | bytes 306142336 | solution.py:210
  539.6 35.6 %fusion.212 = f32[1,1024,6,64]{1,3,2,0:T(8,128)} fusion(f32[6,1024,1024]{1,2,0:T(8,128)} %fusion.209, f32[6,1024,1024]{1,2,0:T(8,128)} %fusion.210, f32[6,1024]{1,0:T(8,128)S(1)} %dynamic-slice_bitcast_fusion.2, pred[1024,1024]{0,1:T(8,128)(4,1)S(1)} %broadcast_compare_fusion.5, bf16[2,1024,6,64]{1,3,2,0:T(8,128)(2,1)} %get-tuple-element.508, ...), kind=kOutput, calls=%fused_computation.45.clone.1 | convolution fusion | flops 874519552 | bytes 105185280 | tf_op jit(solution)/shard_map/while/body/eval_jaxpr/hqk,qhd->khd/dot_general | solution.py:205
  575.2 34.4 %fusion.211 = f32[1,1024,6,64]{1,3,2,0:T(8,128)S(1)} fusion(f32[6,1024,1024]{1,2,0:T(8,128)} %fusion.209, f32[6,1024,1024]{1,2,0:T(8,128)} %fusion.210, f32[6,1024]{1,0:T(8,128)S(1)} %dynamic-slice_bitcast_fusion.2, pred[1024,1024]{0,1:T(8,128)(4,1)S(1)} %broadcast_compare_fusion.5, bf16[2,1024,6,64]{1,3,2,0:T(8,128)(2,1)} %get-tuple-element.506, ...), kind=kOutput, calls=%fused_computation.44.clone.1 | convolution fusion | flops 874519552 | bytes 105185280 | tf_op jit(solution)/shard_map/while/body/eval_jaxpr/hqk,khd->qhd/dot_general | solution.py:202
  614.4 27.5 %dynamic_update_slice.30 = f32[2,1024,6,64]{1,0,3,2:T(2,128)} dynamic-update-slice(f32[2,1024,6,64]{1,0,3,2:T(2,128)} %get-tuple-element.492, f32[1,1024,6,64]{1,0,3,2:T(1,128)S(1)} %copy.200, s32[]{:T(128)S(6)} %copy.221, s32[]{:T(128)} %constant.54.clone.1..sunk, s32[]{:T(128)} %constant.54.clone.1..sunk, s32[]{:T(128)} %constant.54.clone.1..sunk) | dynamic-update-slice | bytes 3145732 | tf_op jit(solution)/shard_map/while/body/jit(dynamic_update_index_in_dim)/dynamic_update_slice | solution.py:210
  641.9 27.5 %dynamic_update_slice.29 = f32[2,1024,6,64]{1,0,3,2:T(2,128)} dynamic-update-slice(f32[2,1024,6,64]{1,0,3,2:T(2,128)} %get-tuple-element.491, f32[1,1024,6,64]{1,0,3,2:T(1,128)S(1)} %copy.199, s32[]{:T(128)S(6)} %copy.221, s32[]{:T(128)} %constant.54.clone.1..sunk, s32[]{:T(128)} %constant.54.clone.1..sunk, s32[]{:T(128)} %constant.54.clone.1..sunk) | dynamic-update-slice | bytes 3145732 | tf_op jit(solution)/shard_map/while/body/jit(dynamic_update_index_in_dim)/dynamic_update_slice | solution.py:210
  708.7 35.7 %fusion.212 = f32[1,1024,6,64]{1,3,2,0:T(8,128)} fusion(f32[6,1024,1024]{1,2,0:T(8,128)} %fusion.209, f32[6,1024,1024]{1,2,0:T(8,128)} %fusion.210, f32[6,1024]{1,0:T(8,128)S(1)} %dynamic-slice_bitcast_fusion.2, pred[1024,1024]{0,1:T(8,128)(4,1)S(1)} %broadcast_compare_fusion.5, bf16[2,1024,6,64]{1,3,2,0:T(8,128)(2,1)} %get-tuple-element.508, ...), kind=kOutput, calls=%fused_computation.45.clone.1 | convolution fusion | flops 874519552 | bytes 105185280 | tf_op jit(solution)/shard_map/while/body/eval_jaxpr/hqk,qhd->khd/dot_general | solution.py:205
  744.4 34.3 %fusion.211 = f32[1,1024,6,64]{1,3,2,0:T(8,128)S(1)} fusion(f32[6,1024,1024]{1,2,0:T(8,128)} %fusion.209, f32[6,1024,1024]{1,2,0:T(8,128)} %fusion.210, f32[6,1024]{1,0:T(8,128)S(1)} %dynamic-slice_bitcast_fusion.2, pred[1024,1024]{0,1:T(8,128)(4,1)S(1)} %broadcast_compare_fusion.5, bf16[2,1024,6,64]{1,3,2,0:T(8,128)(2,1)} %get-tuple-element.506, ...), kind=kOutput, calls=%fused_computation.44.clone.1 | convolution fusion | flops 874519552 | bytes 105185280 | tf_op jit(solution)/shard_map/while/body/eval_jaxpr/hqk,khd->qhd/dot_general | solution.py:202
  783.4 27.5 %dynamic_update_slice.30 = f32[2,1024,6,64]{1,0,3,2:T(2,128)} dynamic-update-slice(f32[2,1024,6,64]{1,0,3,2:T(2,128)} %get-tuple-element.492, f32[1,1024,6,64]{1,0,3,2:T(1,128)S(1)} %copy.200, s32[]{:T(128)S(6)} %copy.221, s32[]{:T(128)} %constant.54.clone.1..sunk, s32[]{:T(128)} %constant.54.clone.1..sunk, s32[]{:T(128)} %constant.54.clone.1..sunk) | dynamic-update-slice | bytes 3145732 | tf_op jit(solution)/shard_map/while/body/jit(dynamic_update_index_in_dim)/dynamic_update_slice | solution.py:210
  810.9 27.5 %dynamic_update_slice.29 = f32[2,1024,6,64]{1,0,3,2:T(2,128)} dynamic-update-slice(f32[2,1024,6,64]{1,0,3,2:T(2,128)} %get-tuple-element.491, f32[1,1024,6,64]{1,0,3,2:T(1,128)S(1)} %copy.199, s32[]{:T(128)S(6)} %copy.221, s32[]{:T(128)} %constant.54.clone.1..sunk, s32[]{:T(128)} %constant.54.clone.1..sunk, s32[]{:T(128)} %constant.54.clone.1..sunk) | dynamic-update-slice | bytes 3145732 | tf_op jit(solution)/shard_map/while/body/jit(dynamic_update_index_in_dim)/dynamic_update_slice | solution.py:210
  989.1 63.4 %reduce-scatter.8.cloned.1.call-done = f32[384,48]{0,1:T(8,128)} async-done(((f32[384,768]{0,1:T(8,128)}), f32[384,48]{0,1:T(8,128)}) %reduce-scatter.8.cloned.1.call-update) | async-done | bytes 73744 | tf_op jit(solution)/shard_map/reduce_scatter | solution.py:234
  1054.1 140.3 %reduce-scatter.10.cloned.1.call-done = f32[48,1536]{1,0:T(8,128)} async-done(((f32[768,1536]{1,0:T(8,128)}), f32[48,1536]{1,0:T(8,128)}) %reduce-scatter.10.cloned.1.call-update) | async-done | bytes 294928 | tf_op jit(solution)/shard_map/reduce_scatter | solution.py:235
  1196.0 141.0 %reduce-scatter.12.cloned.1.call-done = f32[1536,48]{0,1:T(8,128)} async-done(((f32[1536,768]{0,1:T(8,128)}), f32[1536,48]{0,1:T(8,128)}) %reduce-scatter.12.cloned.1.call-update) | async-done | bytes 294928 | tf_op jit(solution)/shard_map/reduce_scatter | solution.py:236
  1338.6 183.0 %all-reduce.11.cloned.1.call-done = f32[3,768,384]{2,0,1:T(4,128)} async-done(((f32[3,768,384]{2,0,1:T(4,128)}), f32[3,768,384]{2,0,1:T(4,128)}) %all-reduce.11.cloned.1.call-update) | async-done | bytes 3538960
  1527.1 120.3 %reduce-scatter.16.cloned.1.call-done = f32[48,8]{1,0:T(8,128)} async-done(((f32[768,8]{1,0:T(8,128)}), f32[48,8]{1,0:T(8,128)}) %reduce-scatter.16.cloned.1.call-update) | async-done | bytes 1552
  1648.8 130.9 %reduce-scatter.14.cloned.1.call-done = f32[128,288]{0,1:T(8,128)} async-done(((f32[128,4608]{0,1:T(8,128)}), f32[128,288]{0,1:T(8,128)}) %reduce-scatter.14.cloned.1.call-update) | async-done | bytes 147472 | tf_op jit(solution)/shard_map/reduce_scatter | solution.py:231
  1792.7 40.0 %psum.39 = f32[]{:T(128)} all-reduce(f32[]{:T(128)S(6)} %add.261), channel_id=1, replica_groups=mesh['dp'=16,'mp'=2] {'dp','mp'}, use_global_device_ids=true, to_apply=%region_34.35 | all-reduce | flops 1 | bytes 8 | tf_op jit(solution)/shard_map/psum | solution.py:253
  (275 shorter events, 506.1 us)
Async XLA Ops:
  7.2 96.6 %all-gather.6.cloned.1.call-start = ((), (), s32[]{:S(2)}) async-start(), calls=%async_computation.5 | async-start | bytes 1253376 | tf_op jit(solution)/shard_map/all_gather | solution.py:103
  8.8 124.7 %all-gather.8.cloned.1.call-start = ((), (), s32[]{:S(2)}) async-start(), calls=%async_computation.6 | async-start | bytes 1880064 | tf_op jit(solution)/shard_map/all_gather | solution.py:105
  10.5 273.7 %all-reduce.7.cloned.1.call-start = ((), (), s32[]{:S(2)}) async-start(), calls=%async_computation.7 | async-start | bytes 12582912 | tf_op jit(solution)/shard_map/psum | solution.py:158
  13.6 106.6 %copy-start.23 = (f32[2048]{0:T(1024)}, f32[2048]{0:T(1024)S(1)}, u32[]{:S(2)}) copy-start(f32[2048]{0:T(1024)S(1)} %broadcast_multiply_fusion.1) | copy-start | bytes 24580
  60.1 60.1 %copy-start.34 = (f32[768]{0:T(1024)}, f32[768]{0:T(1024)S(1)}, u32[]{:S(2)}) copy-start(f32[768]{0:T(1024)S(1)} %get-tuple-element.254) | copy-start | bytes 9220
  60.2 60.1 %copy-start.31 = (f32[2048]{0:T(1024)}, f32[2048]{0:T(1024)S(1)}, u32[]{:S(2)}) copy-start(f32[2048]{0:T(1024)S(1)} %fusion.130) | copy-start | bytes 24580
  60.7 100.9 %copy-start.17 = (f32[1024,32]{0,1:T(8,128)}, f32[1024,32]{0,1:T(8,128)S(1)}, u32[]{:S(2)}) copy-start(f32[1024,32]{0,1:T(8,128)S(1)} %get-tuple-element.336) | copy-start | bytes 393220
  60.7 100.9 %copy-start.19 = (f32[1024,32]{0,1:T(8,128)}, f32[1024,32]{0,1:T(8,128)S(1)}, u32[]{:S(2)}) copy-start(f32[1024,32]{0,1:T(8,128)S(1)} %get-tuple-element.337) | copy-start | bytes 393220
  253.2 98.1 %all-gather.10.cloned.1.call-start = ((), (), s32[]{:S(2)}) async-start(), calls=%async_computation.8 | async-start | bytes 2506752 | tf_op jit(solution)/shard_map/all_gather | solution.py:107
  254.0 162.1 %all-gather.12.cloned.1.call-start = ((), (), s32[]{:S(2)}) async-start(), calls=%async_computation.9 | async-start | bytes 2506752 | tf_op jit(solution)/shard_map/all_gather | solution.py:108
  255.9 216.8 %all-reduce.9.cloned.1.call-start = ((), (), s32[]{:S(2)}) async-start(), calls=%async_computation.10 | async-start | bytes 12582912 | tf_op jit(solution)/shard_map/psum | solution.py:175
  289.7 191.3 %copy-start.25 = (f32[2048]{0:T(1024)}, f32[2048]{0:T(1024)S(1)}, u32[]{:S(2)}) copy-start(f32[2048]{0:T(1024)S(1)} %broadcast_multiply_fusion) | copy-start | bytes 24580
  290.6 190.4 %copy-start.29 = (f32[2048]{0:T(1024)}, f32[2048]{0:T(1024)S(1)}, u32[]{:S(2)}) copy-start(f32[2048]{0:T(1024)S(1)} %fusion.131) | copy-start | bytes 24580
  299.2 116.8 %copy-start.7 = (bf16[2048,768]{1,0:T(8,128)(2,1)S(1)}, bf16[2048,768]{1,0:T(8,128)(2,1)}, u32[]{:S(2)}) copy-start(bf16[2048,768]{1,0:T(8,128)(2,1)} %param.30) | copy-start | bytes 9437188
  441.6 480.6 %all-reduce.13.cloned.1.call-start = ((), (), s32[]{:S(2)}) async-start(), calls=%async_computation.17 | async-start | bytes 25165824 | tf_op jit(solution)/shard_map/psum | solution.py:165
  871.4 181.2 %reduce-scatter.8.cloned.1.call-start = ((), (), s32[]{:S(2)}) async-start(), calls=%async_computation.11 | async-start | bytes 1253376 | tf_op jit(solution)/shard_map/reduce_scatter | solution.py:234
  877.5 316.8 %reduce-scatter.10.cloned.1.call-start = ((), (), s32[]{:S(2)}) async-start(), calls=%async_computation.12 | async-start | bytes 5013504 | tf_op jit(solution)/shard_map/reduce_scatter | solution.py:235
  888.5 448.5 %reduce-scatter.12.cloned.1.call-start = ((), (), s32[]{:S(2)}) async-start(), calls=%async_computation.13 | async-start | bytes 5013504 | tf_op jit(solution)/shard_map/reduce_scatter | solution.py:236
  900.5 621.1 %all-reduce.11.cloned.1.call-start = ((), (), s32[]{:S(2)}) async-start(), calls=%async_computation.16 | async-start | bytes 9437184
  913.3 734.1 %reduce-scatter.16.cloned.1.call-start = ((), (), s32[]{:S(2)}) async-start(), calls=%async_computation.15 | async-start | bytes 417792
  974.2 808.4 %copy-start.4 = (bf16[2048,768]{1,0:T(8,128)(2,1)S(1)}, bf16[2048,768]{1,0:T(8,128)(2,1)}, u32[]{:S(2)}) copy-start(bf16[2048,768]{1,0:T(8,128)(2,1)} %param.27) | copy-start | bytes 9437188
  974.2 805.6 %reduce-scatter.14.cloned.1.call-start = ((), (), s32[]{:S(2)}) async-start(), calls=%async_computation.14 | async-start | bytes 2506752 | tf_op jit(solution)/shard_map/reduce_scatter | solution.py:231
  1782.6 54.4 %copy-start.28 = (f32[384,48]{0,1:T(8,128)S(1)}, f32[384,48]{0,1:T(8,128)}, u32[]{:S(2)}) copy-start(f32[384,48]{0,1:T(8,128)} %param.41) | copy-start | bytes 221188
  1782.6 58.0 %copy-start.22 = (f32[48,1536]{1,0:T(8,128)S(1)}, f32[48,1536]{1,0:T(8,128)}, u32[]{:S(2)}) copy-start(f32[48,1536]{1,0:T(8,128)} %param.44) | copy-start | bytes 884740
  (43 other events, 435.6 us)
Sparse Core Ops, SparseCore 0:
  11.4 59.7 all-gather.5
  74.5 58.9 all-gather.7
  253.3 30.7 all-reduce.6
  287.8 63.4 all-gather.9
  354.9 61.0 all-gather.11
  441.7 30.8 all-reduce.8
  871.5 50.6 all-reduce.12
  927.0 125.5 reduce-scatter.7
  1057.8 136.5 reduce-scatter.9
  1200.2 136.7 reduce-scatter.11
  1342.7 178.8 all-reduce.10
  1526.8 120.5 reduce-scatter.15
  1652.3 127.3 reduce-scatter.13
where the time goes:
time: 1860 us; the launch traced here: 1850 us
  waiting for transfers between devices  947 us (51%)
  matrix products  399 us (21%)
  other arithmetic  180 us (10%)
  local copies, waits for them, and re-layouts  178 us (10%)
  blocking collectives  126 us (7%)
  between operations  22.2 us (1%)
    unnamed x15, waiting for transfers between devices  303 us
    reduce_scatter x1, waiting for transfers between devices, per_device(): lax.psum_scatter(grad_down, 'dp', scatter_dimension=1, tiled=True)  141 us
    reduce_scatter x1, waiting for transfers between devices, per_device(): lax.psum_scatter(grad_up, 'dp', scatter_dimension=0, tiled=True)  140 us
    reduce_scatter x1, waiting for transfers between devices, per_device(): lax.psum_scatter(grad_ada, 'dp', scatter_dimension=1, tiled=True)  131 us
    dynamic_update_slice x8, local copies, waits for them, and re-layouts, per_device(): lax.map(attend_back, (queries, keys, values, segments, logsums, grad_atte...  119 us
    dot_general x2, matrix products, attend_back(): jnp.einsum('hqk,qhd->khd', grad_scores, query_block, preferred_element_ty...  71.3 us
    dot_general x2, matrix products, attend_back(): jnp.einsum('hqk,khd->qhd', grad_scores, key_block, preferred_element_type...  68.8 us
    reduce_scatter x1, waiting for transfers between devices, per_device(): lax.psum_scatter(grad_out, 'dp', scatter_dimension=1, tiled=True)  63.4 us
  transfers between devices with their start and end apart: 13, of which 12 were waited for; matrix products, arithmetic and copies ran while one was open for 10% of the time, Pallas kernels for 0%

commit v1 on v0

v1 whole, which is shorter than its diff:
```python
import functools
import math

import jax
import jax.numpy as jnp
from jax import lax
from jax.experimental import pallas as pl
from jax.experimental.pallas import tpu as pltpu
from jax.sharding import PartitionSpec as P

HEAD_DIM = 64
LANES = 128
MASKED = -1e30
ROW_BLOCK = 256
VMEM_LIMIT = 64_000_000
clip_limit = 1.0
step_rates = (0.075, 0.75, 0.075, 0.25, 0.075, 0.075)
decay_rates = (0.01, 0.0, 0.01, 0.01, 0.01, 0.01)

F32 = jnp.float32
BF = jnp.bfloat16
NN = (((1,), (0,)), ((), ()))
NT = (((1,), (1,)), ((), ()))


def dot(left, right, dims=NN):
    return lax.dot_general(left, right, dims, preferred_element_type=F32)


def shape_of(shape, dtype):
    return jax.ShapeDtypeStruct(shape, dtype)


def resident(shape, index):
    return pl.BlockSpec(shape, lambda *_: index, pipeline_mode=pl.Buffered(1))


def params():
    return pltpu.CompilerParams(vmem_limit_bytes=VMEM_LIMIT)


def adam_update(weight, first, second, grad, clip_factor, fix_one, fix_two, rate, decay):
    clipped = grad * clip_factor
    first_new = 0.9 * first + 0.1 * clipped
    second_new = 0.999 * second + 0.001 * clipped * clipped
    update = first_new / fix_one / (jnp.sqrt(second_new / fix_two) + 1e-08) + decay * weight
    return (weight - rate * update, first_new, second_new)


def rope_tables(length):
    half = HEAD_DIM // 2
    inverse = jnp.exp(jnp.arange(half, dtype=F32) * (-2.0 * math.log(10000.0) / HEAD_DIM))
    angles = jnp.arange(length, dtype=F32)[:, None] * inverse[None, :]
    cosines, sines = jnp.cos(angles), jnp.sin(angles)
    return (
        jnp.concatenate([cosines] * 4, axis=1),
        jnp.concatenate([-sines, sines, -sines, sines], axis=1),
    )


def swap_halves(values):
    width = values.shape[1]
    lane = lax.broadcasted_iota(jnp.int32, values.shape, 1)
    ahead = pltpu.roll(values, width - HEAD_DIM // 2, 1)
    behind = pltpu.roll(values, HEAD_DIM // 2, 1)
    return jnp.where(lane % HEAD_DIM < HEAD_DIM // 2, ahead, behind)


def silu_low(cond):
    value = cond.astype(F32)
    return (value / (1.0 + jnp.exp(-value))).astype(BF)


def normalize(rows):
    centre = rows - jnp.mean(rows, axis=-1, keepdims=True)
    scale = lax.rsqrt(jnp.mean(centre * centre, axis=-1, keepdims=True) + 1e-05)
    return centre * scale, scale


def norm_backward(grad, normal, scale):
    return scale * (
        grad
        - jnp.mean(grad, axis=-1, keepdims=True)
        - normal * jnp.mean(grad * normal, axis=-1, keepdims=True)
    )


def cond_rows(cond):
    return jnp.concatenate([cond.T, jnp.ones((16, cond.shape[0]), BF)], axis=0)


def first_kernel(half, x_ref, c_ref, wa_ref, p_ref, wqa_ref, wqb_ref, cos_ref, sin_ref,
                 h_ref, q_ref, k_ref, v_ref):
    width = x_ref.shape[1]
    own = width // 2
    cond = silu_low(c_ref[...])
    mod = dot(cond, wa_ref[0 : 2 * width, :], NT)
    shift = mod[:, :width] + p_ref[2:3, :]
    scale = mod[:, width:] + p_ref[3:4, :]
    normal, _ = normalize(x_ref[...].astype(F32))
    h = (normal * p_ref[0:1, :] * (1.0 + scale) + shift).astype(BF)
    h_ref[...] = h
    cos = jnp.concatenate([cos_ref[...]] * (own // LANES), axis=1)
    sin = jnp.concatenate([sin_ref[...]] * (own // LANES), axis=1)
    for start, w_ref in ((0, wqa_ref), (own, wqb_ref)):
        cols = slice(start, start + own)
        query = dot(h, w_ref[:, 0:own])
        query = query * cos + swap_halves(query) * sin
        q_ref[:, cols] = (query * HEAD_DIM**-0.5).astype(BF)
        key = dot(h, w_ref[:, own : 2 * own])
        k_ref[:, cols] = (key * cos + swap_halves(key) * sin).astype(BF)
        v_ref[:, cols] = dot(h, w_ref[:, 2 * own :]).astype(BF)


def first_stage(half, tokens, cond, wa, norms, near, far, tables):
    width = tokens.shape[1]
    rows = tables[0].shape[0]
    blocks = rows // ROW_BLOCK
    mine = lambda i, half: (half[0] * blocks + i, 0)
    plain = lambda i, half: (i, 0)
    row = pl.BlockSpec((ROW_BLOCK, width), plain)
    return pl.pallas_call(
        first_kernel,
        grid_spec=pltpu.PrefetchScalarGridSpec(
            num_scalar_prefetch=1,
            grid=(blocks,),
            in_specs=[
                pl.BlockSpec((ROW_BLOCK, width), mine),
                pl.BlockSpec((ROW_BLOCK, cond.shape[1]), mine),
                resident(wa.shape, (0, 0)),
                resident(norms.shape, (0, 0)),
                resident((width, 3 * width // 2), (0, 0)),
                resident((width, 3 * width // 2), (0, 0)),
                pl.BlockSpec((ROW_BLOCK, LANES), plain),
                pl.BlockSpec((ROW_BLOCK, LANES), plain),
            ],
            out_specs=[row] * 4,
        ),
        out_shape=[shape_of((rows, width), BF)] * 4,
        compiler_params=params(),
        name="first_stage",
    )(half, tokens, cond, wa, norms, near, far, *tables)


def split_heads(pair, other):
    low = lax.broadcasted_iota(jnp.int32, pair.shape, 1) < HEAD_DIM
    return jnp.where(low, pair, other), jnp.where(low, other, pair)


def attend_kernel(lo_ref, hi_ref, q_ref, k_ref, v_ref, fq_ref, fk_ref, o_ref, lse_ref,
                  qz, kz, vt, *, bq, bk):
    length = q_ref.shape[0]
    qz[0], qz[1] = split_heads(q_ref[...], fq_ref[...])
    kz[0], kz[1] = split_heads(k_ref[...], fk_ref[...])
    vt[...] = v_ref[...].T

    def query_block(i, _):
        off = pl.multiple_of(i * bq, bq)
        queries = [qz[h, pl.ds(off, bq), :] for h in range(2)]

        def key_block(j, carry):
            koff = pl.multiple_of(j * bk, bk)
            scores = [dot(kz[h, pl.ds(koff, bk), :], queries[h], NT) for h in range(2)]
            out = []
            for h in range(2):
                top, total, mixed = carry[3 * h : 3 * h + 3]
                new_top = jnp.maximum(top, jnp.max(scores[h], axis=0, keepdims=True))
                weights = jnp.exp(scores[h] - new_top)
                fade = jnp.exp(top - new_top)
                total = total * fade + jnp.sum(weights, axis=0, keepdims=True)
                values = vt[HEAD_DIM * h : HEAD_DIM * (h + 1), pl.ds(koff, bk)]
                mixed = mixed * fade + dot(values, weights.astype(BF))
                out += [new_top, total, mixed]
            return tuple(out)

        start = (
            jnp.full((1, bq), -3e38, F32),
            jnp.zeros((1, bq), F32),
            jnp.zeros((HEAD_DIM, bq), F32),
        )
        done = lax.fori_loop(lo_ref[i], hi_ref[i], key_block, start * 2)
        mixed = jnp.concatenate([done[2] / done[1], done[5] / done[4]], axis=0)
        o_ref[pl.ds(off, bq), :] = mixed.T.astype(BF)
        lse_ref[0, 0:1, pl.ds(off, bq)] = done[0] + jnp.log(done[1])
        lse_ref[0, 1:2, pl.ds(off, bq)] = done[3] + jnp.log(done[4])
        return 0

    lax.fori_loop(0, length // bq, query_block, 0)


def block_ranges(segment, block, other):
    first, last = segment[::block], segment[block - 1 :: block]
    low = jnp.sum(segment[None, :] < first[:, None], axis=1)
    high = jnp.sum(segment[None, :] <= last[:, None], axis=1)
    return (low // other).astype(jnp.int32), ((high + other - 1) // other).astype(jnp.int32)


def document_features(segment):
    lane = lax.broadcasted_iota(jnp.int32, (segment.shape[0], LANES), 1) % HEAD_DIM
    same = lane == segment[:, None]
    query = jnp.where(same, 1.0, 0.0).astype(BF)
    key = jnp.where((lane < 4) & ~same, MASKED, 0.0).astype(BF)
    return query, key


def attend(queries, keys, values, segment, features, bq=1024, bk=512):
    length, width = queries.shape
    bq, bk = min(bq, length), min(bk, length)
    pairs = width // LANES
    low, high = block_ranges(segment, bq, bk)
    pair = pl.BlockSpec((length, LANES), lambda p, *_: (0, p))
    fixed = pl.BlockSpec((length, LANES), lambda p, *_: (0, 0))
    scratch = pltpu.VMEM((2, length, LANES), BF)
    return pl.pallas_call(
        functools.partial(attend_kernel, bq=bq, bk=bk),
        grid_spec=pltpu.PrefetchScalarGridSpec(
            num_scalar_prefetch=2,
            grid=(pairs,),
            in_specs=[pair, pair, pair, fixed, fixed],
            out_specs=[pair, pl.BlockSpec((1, 2, length), lambda p, *_: (p, 0, 0))],
            scratch_shapes=[scratch, scratch, pltpu.VMEM((LANES, length), BF)],
        ),
        out_shape=[shape_of((length, width), BF), shape_of((pairs, 2, length), F32)],
        compiler_params=params(),
        name="attend",
    )(low, high, queries, keys, values, *features)


def attend_back_kernel(lo_ref, hi_ref, q_ref, k_ref, v_ref, do_ref, o_ref, lse_ref, fq_ref,
                       fk_ref, cos_ref, sin_ref, dq_ref, dk_ref, dv_ref,
                       qz, kz, qm, dm, vm, kt, delta, dqt, *, bq, bk):
    length = q_ref.shape[0]
    zero = jnp.zeros((length, LANES), BF)
    qz[0], qz[1] = split_heads(q_ref[...], fq_ref[...])
    kz[0], kz[1] = split_heads(k_ref[...], fk_ref[...])
    qm[0], qm[1] = split_heads(q_ref[...], zero)
    dm[0], dm[1] = split_heads(do_ref[...], zero)
    vm[0], vm[1] = split_heads(v_ref[...], zero)
    kt[...] = k_ref[...].T
    product = (do_ref[...].astype(F32) * o_ref[...].astype(F32)).T
    delta[0:1, :] = jnp.sum(product[:HEAD_DIM], axis=0, keepdims=True)
    delta[1:2, :] = jnp.sum(product[HEAD_DIM:], axis=0, keepdims=True)
    dqt[...] = jnp.zeros_like(dqt)

    def unrotate(grad, off, rows):
        cos, sin = cos_ref[pl.ds(off, rows), :], sin_ref[pl.ds(off, rows), :]
        return (grad * cos - swap_halves(grad) * sin).astype(BF)

    def key_block(j, _):
        koff = pl.multiple_of(j * bk, bk)
        keys = [kz[h, pl.ds(koff, bk), :] for h in range(2)]
        values = [vm[h, pl.ds(koff, bk), :] for h in range(2)]

        def query_block(i, carry):
            dk, dv = carry
            off = pl.multiple_of(i * bq, bq)
            scores = [dot(keys[h], qz[h, pl.ds(off, bq), :], NT) for h in range(2)]
            grads = [dot(values[h], dm[h, pl.ds(off, bq), :], NT) for h in range(2)]
            for h in range(2):
                weights = jnp.exp(scores[h] - lse_ref[0, h : h + 1, pl.ds(off, bq)])
                dv = dv + dot(weights.astype(BF), dm[h, pl.ds(off, bq), :])
                ds = (weights * (grads[h] - delta[h : h + 1, pl.ds(off, bq)])).astype(BF)
                dk = dk + dot(ds, qm[h, pl.ds(off, bq), :])
                head = slice(HEAD_DIM * h, HEAD_DIM * (h + 1))
                dqt[head, pl.ds(off, bq)] += dot(kt[head, pl.ds(koff, bk)], ds)
            return dk, dv

        zeros = jnp.zeros((bk, LANES), F32)
        dk, dv = lax.fori_loop(lo_ref[j], hi_ref[j], query_block, (zeros, zeros))
        dk_ref[pl.ds(koff, bk), :] = unrotate(dk, koff, bk)
        dv_ref[pl.ds(koff, bk), :] = dv.astype(BF)
        return 0

    lax.fori_loop(0, length // bk, key_block, 0)
    dq_ref[...] = unrotate(dqt[...].T * HEAD_DIM**-0.5, 0, length)


def attend_back(queries, keys, values, upstream, mixed, lse, segment, features, tables,
                bq=512, bk=256):
    length, width = queries.shape
    bq, bk = min(bq, length), min(bk, length)
    pairs = width // LANES
    low, high = block_ranges(segment, bk, bq)
    pair = pl.BlockSpec((length, LANES), lambda p, *_: (0, p))
    fixed = pl.BlockSpec((length, LANES), lambda p, *_: (0, 0))
    scratch = pltpu.VMEM((2, length, LANES), BF)
    return pl.pallas_call(
        functools.partial(attend_back_kernel, bq=bq, bk=bk),
        grid_spec=pltpu.PrefetchScalarGridSpec(
            num_scalar_prefetch=2,
            grid=(pairs,),
            in_specs=[pair] * 5
            + [pl.BlockSpec((1, 2, length), lambda p, *_: (p, 0, 0))]
            + [fixed] * 4,
            out_specs=[pair] * 3,
            scratch_shapes=[scratch] * 5
            + [
                pltpu.VMEM((LANES, length), BF),
                pltpu.VMEM((8, length), F32),
                pltpu.VMEM((LANES, length), F32),
            ],
        ),
        out_shape=[shape_of((length, width), BF)] * 3,
        compiler_params=params(),
        name="attend_back",
    )(low, high, queries, keys, values, upstream, mixed, lse, *features, *tables)


def middle_kernel(half, x_ref, g_ref, c_ref, o_ref, wa_ref, p_ref, woa_ref, wob_ref, w1a_ref,
                  w1b_ref, w2a_ref, w2b_ref,
                  res_ref, dx_ref, do_ref, z_ref, gy_ref, h_ref, du_ref, ga_ref, dwa_ref,
                  dp_ref, slope, *, chunk):
    width = x_ref.shape[1]
    own = width // 2
    hidden = w1a_ref.shape[1]
    cond = silu_low(c_ref[...])

    def modulation(block):
        rows = wa_ref[block * width : (block + 1) * width, :]
        return dot(cond, rows, NT) + p_ref[block + 2 : block + 3, :]

    gate_one, shift, scale, gate_two = (modulation(block) for block in (2, 3, 4, 5))
    branch = dot(o_ref[:, :own], woa_ref[...], NT) + dot(o_ref[:, own:], wob_ref[...], NT)
    middle = x_ref[...].astype(F32) + gate_one * branch
    normal, rstd = normalize(middle)
    gain = p_ref[1:2, :]
    spread = 1.0 + scale
    h = (normal * gain * spread + shift).astype(BF)
    h_ref[...] = h

    out = jnp.zeros_like(middle)
    for start, up_ref, down_ref in ((0, w1a_ref, w2a_ref), (hidden, w1b_ref, w2b_ref)):
        for at in range(0, hidden, chunk):
            u = dot(h, up_ref[:, at : at + chunk])
            square = u * u
            flat = jnp.tanh(math.sqrt(2.0 / math.pi) * u * (1.0 + 0.044715 * square))
            half_up = 0.5 * (1.0 + flat)
            z = (u * half_up).astype(BF)
            z_ref[:, start + at : start + at + chunk] = z
            slope[:, start + at : start + at + chunk] = half_up + 0.5 * u * (
                1.0 - flat * flat
            ) * (math.sqrt(2.0 / math.pi) * (1.0 + 3.0 * 0.044715 * square))
            out = out + dot(z, down_ref[:, at : at + chunk], NT)

    g = g_ref[...].astype(F32)
    res_ref[...] = (middle + gate_two * out).astype(BF)
    gy = (gate_two * g).astype(BF)
    gy_ref[...] = gy
    dgate_two = (g * out).astype(BF)

    dh = jnp.zeros_like(middle)
    for start, up_ref, down_ref in ((0, w1a_ref, w2a_ref), (hidden, w1b_ref, w2b_ref)):
        for at in range(0, hidden, chunk):
            dz = dot(gy, down_ref[:, at : at + chunk])
            du = (dz * slope[:, start + at : start + at + chunk]).astype(BF)
            du_ref[:, start + at : start + at + chunk] = du
            dh = dh + dot(du, up_ref[:, at : at + chunk], NT)

    dn = dh * normal
    dx = g + norm_backward(dh * gain * spread, normal, rstd)
    dx_ref[...] = dx
    ga = (gate_one * dx).astype(BF)
    ga_ref[...] = ga
    do_ref[:, :own] = dot(ga, woa_ref[...]).astype(BF)
    do_ref[:, own:] = dot(ga, wob_ref[...]).astype(BF)

    @pl.when(pl.program_id(0) == 0)
    def _():
        dwa_ref[...] = jnp.zeros_like(dwa_ref)
        dp_ref[...] = jnp.zeros_like(dp_ref)

    rows = cond_rows(cond)
    grads = ((dx * branch).astype(BF), dh.astype(BF), (dn * gain).astype(BF), dgate_two)
    for block, grad in enumerate(grads):
        dwa_ref[:, block * width : (block + 1) * width] += dot(rows, grad)
    dp_ref[0:1, :] += jnp.sum(dn * spread, axis=0, keepdims=True)


def middle_stage(half, tokens, out_grad, cond, mixed, wa, norms, near, far, wide_near, wide_far):
    width = tokens.shape[1]
    rows = mixed.shape[0]
    hidden = wide_near.shape[1] // 2
    blocks = rows // ROW_BLOCK
    mine = lambda i, half: (half[0] * blocks + i, 0)
    plain = lambda i, half: (i, 0)
    row = pl.BlockSpec((ROW_BLOCK, width), plain)
    wide = pl.BlockSpec((ROW_BLOCK, 2 * hidden), plain)
    narrow = shape_of((rows, width), BF)
    broad = shape_of((rows, 2 * hidden), BF)
    total = (cond.shape[1] + 16, 4 * width)
    return pl.pallas_call(
        functools.partial(middle_kernel, chunk=768),
        grid_spec=pltpu.PrefetchScalarGridSpec(
            num_scalar_prefetch=1,
            grid=(blocks,),
            in_specs=[
                pl.BlockSpec((ROW_BLOCK, width), mine),
                pl.BlockSpec((ROW_BLOCK, width), mine),
                pl.BlockSpec((ROW_BLOCK, cond.shape[1]), mine),
                row,
                resident(wa.shape, (0, 0)),
                resident(norms.shape, (0, 0)),
                resident((width, width // 2), (0, 3)),
                resident((width, width // 2), (0, 3)),
                resident((width, hidden), (0, 0)),
                resident((width, hidden), (0, 0)),
                resident((width, hidden), (0, 1)),
                resident((width, hidden), (0, 1)),
            ],
            out_specs=[row, row, row, wide, row, row, wide, row,
                       pl.BlockSpec(total, lambda i, half: (0, 0)),
                       pl.BlockSpec((8, width), lambda i, half: (0, 0))],
            scratch_shapes=[pltpu.VMEM((ROW_BLOCK, 2 * hidden), F32)],
        ),
        out_shape=[narrow, shape_of((rows, width), F32), narrow, broad, narrow, narrow, broad,
                   narrow, shape_of(total, F32), shape_of((8, width), F32)],
        compiler_params=params(),
        name="middle_stage",
    )(half, tokens, out_grad, cond, mixed, wa, norms, near, far, wide_near, wide_far,
      wide_near, wide_far)


def last_kernel(half, x_ref, c_ref, dx_ref, dq_ref, dk_ref, dv_ref, wa_ref, p_ref, wqa_ref,
                wqb_ref, out_ref, dwa_ref, dp_ref):
    width = x_ref.shape[1]
    own = width // 2
    cond = silu_low(c_ref[...])
    scale = dot(cond, wa_ref[width : 2 * width, :], NT) + p_ref[3:4, :]
    dh = jnp.zeros(x_ref.shape, F32)
    for start, w_ref in ((0, wqa_ref), (own, wqb_ref)):
        cols = slice(start, start + own)
        for index, grad_ref in enumerate((dq_ref, dk_ref, dv_ref)):
            dh = dh + dot(grad_ref[:, cols], w_ref[:, index * own : (index + 1) * own], NT)
    normal, rstd = normalize(x_ref[...].astype(F32))
    gain = p_ref[0:1, :]
    spread = 1.0 + scale
    dn = dh * normal
    out_ref[...] = dx_ref[...] + norm_backward(dh * gain * spread, normal, rstd)

    @pl.when(pl.program_id(0) == 0)
    def _():
        dwa_ref[...] = jnp.zeros_like(dwa_ref)
        dp_ref[...] = jnp.zeros_like(dp_ref)

    rows = cond_rows(cond)
    dwa_ref[:, :width] += dot(rows, dh.astype(BF))
    dwa_ref[:, width:] += dot(rows, (dn * gain).astype(BF))
    dp_ref[0:1, :] += jnp.sum(dn * spread, axis=0, keepdims=True)


def last_stage(half, tokens, cond, dx, grads, wa, norms, near, far):
    width = tokens.shape[1]
    rows = dx.shape[0]
    blocks = rows // ROW_BLOCK
    mine = lambda i, half: (half[0] * blocks + i, 0)
    row = pl.BlockSpec((ROW_BLOCK, width), lambda i, half: (i, 0))
    total = (cond.shape[1] + 16, 2 * width)
    return pl.pallas_call(
        last_kernel,
        grid_spec=pltpu.PrefetchScalarGridSpec(
            num_scalar_prefetch=1,
            grid=(blocks,),
            in_specs=[
                pl.BlockSpec((ROW_BLOCK, width), mine),
                pl.BlockSpec((ROW_BLOCK, cond.shape[1]), mine),
                row, row, row, row,
                resident(wa.shape, (0, 0)),
                resident(norms.shape, (0, 0)),
                resident((width, 3 * width // 2), (0, 0)),
                resident((width, 3 * width // 2), (0, 0)),
            ],
            out_specs=[row, pl.BlockSpec(total, lambda i, half: (0, 0)),
                       pl.BlockSpec((8, width), lambda i, half: (0, 0))],
        ),
        out_shape=[shape_of((rows, width), F32), shape_of(total, F32), shape_of((8, width), F32)],
        compiler_params=params(),
        name="last_stage",
    )(half, tokens, cond, dx, *grads, wa, norms, near, far)


def weight_grad_kernel(*refs, plan):
    lefts, rights = plan["lefts"], plan["rights"]
    left_refs, right_refs = refs[:lefts], refs[lefts : lefts + rights]
    out_ref, turned = refs[lefts + rights :]
    step = pl.program_id(0)
    for begin, end, left, right in plan["spans"]:

        @pl.when(step == begin)
        def _():
            turned[...] = left_refs[left][...].T

        @pl.when((step >= begin) & (step < end))
        def _():
            out_ref[...] = dot(turned[...], right_refs[right][...]).astype(BF)


def weight_grads(lefts, rights, spans, block, name):
    rows, width = lefts[0].shape
    begin, plan, maps = 0, [], []
    for steps, left, right, first in spans:
        plan.append((begin, begin + steps, left, right))
        maps.append((begin, steps, first))
        begin += steps

    def column_map(begin, steps, first):
        return lambda i: (0, first + jnp.clip(i - begin, 0, steps - 1))

    return pl.pallas_call(
        functools.partial(
            weight_grad_kernel,
            plan={"lefts": len(lefts), "rights": len(rights), "spans": plan},
        ),
        grid=(begin,),
        in_specs=[resident((rows, width), (0, 0))] * len(lefts)
        + [pl.BlockSpec((rows, block), column_map(*entry)) for entry in maps],
        out_specs=pl.BlockSpec((width, block), lambda i: (0, i)),
        out_shape=shape_of((width, begin * block), BF),
        scratch_shapes=[pltpu.VMEM((width, rows), BF)],
        compiler_params=params(),
        name=name,
    )(*lefts, *rights)


def factors(count):
    return (count // 4, 2, 2)


def swap_mp(value):
    return lax.ppermute(value, "mp", [(0, 1), (1, 0)])


def swap_dp(value, distance):
    count = lax.axis_size("dp")
    return lax.ppermute(value, "dp", [(i, i ^ distance) for i in range(count)])


def turn_dp(value, distance):
    count = lax.axis_size("dp")
    return lax.ppermute(value, "dp", [(i, (i + distance) % count) for i in range(count)])


def pick(value, index, axis):
    return lax.dynamic_index_in_dim(value, index, axis, keepdims=False)


def scatter_sum(parts, order):
    count = lax.axis_size("dp")
    outer, mid, inner = factors(count)
    me = lax.axis_index("dp")
    place = {4: me // 4, 2: (me // 2) % 2, 1: me % 2}

    def widen(part):
        return part.reshape((outer, mid, inner) + part.shape[1:]).astype(F32)

    total = widen(parts[0])
    for part in parts[1:]:
        total = total + widen(part)
    for distance in order:
        axis = 1 if (distance == 2 or total.ndim == 4) else 2
        gone = pick(total, 1 - place[distance], axis).astype(BF)
        total = pick(total, place[distance], axis) + swap_dp(gone, distance).astype(F32)
    arrived = [
        turn_dp(pick(total, (place[4] + hop) % outer, 0).astype(BF), 4 * hop)
        for hop in range(1, outer)
    ]
    total = pick(total, place[4], 0)
    for piece in arrived:
        total = total + piece.astype(F32)
    return total


def scatter_halves(near, far_sum):
    count = lax.axis_size("dp")
    width, columns = near.shape
    cut = columns // 2 // LANES * LANES
    shards = lambda value: value.reshape(count, width // count, value.shape[1])
    first = scatter_sum([shards(near[:, :cut]), shards(far_sum[:, :cut])], (2, 1))
    second = scatter_sum([shards(near[:, cut:]), shards(far_sum[:, cut:])], (1, 2))
    return jnp.concatenate([first, second], axis=1)


def sum_everywhere(value):
    value = value + swap_mp(value)
    distance = 1
    while distance < lax.axis_size("dp"):
        value = value + swap_dp(value, distance)
        distance *= 2
    return value


def in_order(half, near, far):
    first = jnp.where(half == 0, near, far)
    second = jnp.where(half == 0, far, near)
    return jnp.concatenate([first, second], axis=0)


def per_device(
    tokens, cond, segments, out_grad, step,
    ada_weight, ada_first, ada_second,
    norm_params, norm_first, norm_second,
    qkv_weight, qkv_first, qkv_second,
    out_weight, out_first, out_second,
    up_weight, up_first, up_second,
    down_weight, down_first, down_second,
):
    count = lax.axis_size("dp")
    width = tokens.shape[1]
    rows = tokens.shape[0] // 2
    conds = cond.shape[1]
    part = width // count
    half = lax.axis_index("mp")
    half_ref = half.reshape(1).astype(jnp.int32)
    token_total = float(tokens.shape[0] * count)

    ada_shard = ada_weight.T.astype(BF)
    qkv_shard = qkv_weight.astype(BF).transpose(1, 0, 2).reshape(part, -1)
    near_shard = jnp.concatenate([qkv_shard, out_weight.astype(BF).T], axis=1)
    wide_shard = jnp.concatenate([up_weight.astype(BF), down_weight.astype(BF).T], axis=1)
    wa = lax.all_gather(ada_shard, "dp", axis=0, tiled=True)
    norms = lax.all_gather(norm_params.astype(BF), "dp", axis=1, tiled=True).astype(F32)
    near = lax.all_gather(near_shard, "dp", axis=0, tiled=True)
    far = swap_mp(near)
    wide_near = lax.all_gather(wide_shard, "dp", axis=0, tiled=True)
    wide_far = swap_mp(wide_near)

    segment = pick(segments, half, 0)
    features = document_features(segment)
    tables = rope_tables(rows)

    h_one, queries, keys, values = first_stage(
        half_ref, tokens, cond, wa, norms, near, far, tables
    )
    mixed, lse = attend(queries, keys, values, segment, features)
    result, dx, upstream, z, gy, h_two, du, ga, dwa_two, dp_two = middle_stage(
        half_ref, tokens, out_grad, cond, mixed, wa, norms, near, far, wide_near, wide_far
    )
    result_far = swap_mp(result)

    block = width // 2
    steps = du.shape[1] // 2 // block

    def middle_grads(which, name):
        return weight_grads(
            [gy, h_two, ga], [du, z, mixed],
            [(steps, 1, 0, which * steps), (steps, 0, 1, which * steps), (1, 2, 2, which)],
            block, name,
        )

    middle_far = swap_mp(middle_grads(1, "middle_grads_far"))
    middle_near = middle_grads(0, "middle_grads_near")
    middle_sum = scatter_halves(middle_near, middle_far)

    grads = attend_back(queries, keys, values, upstream, mixed, lse, segment, features, tables)

    def first_grads(which, name):
        return weight_grads(
            [h_one], list(grads), [(1, 0, index, which) for index in range(3)], block, name
        )

    first_far = swap_mp(first_grads(1, "first_grads_far"))
    first_near = first_grads(0, "first_grads_near")
    first_sum = scatter_halves(first_near, first_far)

    input_grad, dwa_one, dp_one = last_stage(
        half_ref, tokens, cond, dx, grads, wa, norms, near, far
    )
    input_far = swap_mp(input_grad)

    dwa = jnp.concatenate([dwa_one, dwa_two], axis=1)
    ada_cols = dwa.shape[1] // count
    dwa_rows = dwa[:conds].T.astype(BF).reshape(count, 2, ada_cols // 2, conds)
    ada_near, ada_far = pick(dwa_rows, half, 1), swap_mp(pick(dwa_rows, 1 - half, 1))
    ada_half = scatter_sum([ada_near, ada_far], (2, 1))
    norm_rows = jnp.concatenate(
        [dp_one[0:1], dp_two[0:1], dwa[conds].reshape(6, width)], axis=0
    )
    norm_sum = lax.psum_scatter(
        norm_rows + swap_mp(norm_rows), "dp", scatter_dimension=1, tiled=True
    )

    wide_cols = du.shape[1] // 2
    up_mean = middle_sum[:, :wide_cols] / token_total
    down_mean = middle_sum[:, wide_cols : 2 * wide_cols] / token_total
    out_mean = middle_sum[:, 2 * wide_cols :] / token_total
    qkv_mean = first_sum / token_total
    ada_mean = ada_half / token_total
    norm_mean = norm_sum / token_total
    local_sq = (
        jnp.sum(qkv_mean * qkv_mean)
        + jnp.sum(out_mean * out_mean)
        + jnp.sum(up_mean * up_mean)
        + jnp.sum(down_mean * down_mean)
        + jnp.sum(ada_mean * ada_mean)
        + 0.5 * jnp.sum(norm_mean * norm_mean)
    )
    grad_norm = jnp.sqrt(sum_everywhere(jnp.full((8, LANES), local_sq, F32))[0, 0])
    clip_factor = jnp.minimum(1.0, clip_limit / (grad_norm + 1e-06))
    step_count = step[0].astype(F32)
    fix_one = 1.0 - jnp.exp(step_count * math.log(0.9))
    fix_two = 1.0 - jnp.exp(step_count * math.log(0.999))

    ada_grad = in_order(half, ada_mean, swap_mp(ada_mean)).T
    qkv_grad = qkv_mean.reshape(part, 3, -1).transpose(1, 0, 2)
    state = (
        (ada_weight, ada_first, ada_second, ada_grad),
        (norm_params, norm_first, norm_second, norm_mean),
        (qkv_weight, qkv_first, qkv_second, qkv_grad),
        (out_weight, out_first, out_second, out_mean.T),
        (up_weight, up_first, up_second, up_mean),
        (down_weight, down_first, down_second, down_mean.T),
    )
    outputs = [
        in_order(half, result, result_far),
        in_order(half, input_grad, input_far),
        grad_norm.reshape(1),
    ]
    for index, entry in enumerate(state):
        outputs += adam_update(
            *entry, clip_factor, fix_one, fix_two, step_rates[index], decay_rates[index]
        )
    return tuple(outputs)


def solution(mesh):
    column = (P(None, "dp"),) * 3
    weights = (
        column
        + column
        + (P(None, "dp", "mp"),) * 3
        + (P("mp", "dp"),) * 3
        + (P("dp", "mp"),) * 3
        + (P("mp", "dp"),) * 3
    )
    row = P("dp", None)
    return jax.shard_map(
        per_device,
        mesh=mesh,
        in_specs=(row, row, row, row, P()) + weights,
        out_specs=(row, row, P()) + weights,
        check_vma=False,
    )
```

time: 1860 us -> 667 us (0.36)
  waiting for transfers between devices: 947 us -> 311 us
  matrix products: 399 us -> 0 us
  Pallas kernels: 0 us -> 188 us
  local copies, waits for them, and re-layouts: 178 us -> 17.1 us
  other arithmetic: 180 us -> 44.1 us
  blocking collectives: 126 us -> 38.8 us
  starting transfers between devices: 1 us -> 37.5 us
    reduce_scatter x4 -> x0, waiting for transfers between devices: 476 us -> none  [the longest x1 141 us: per_device(): lax.psum_scatter(grad_down, 'dp', scatter_dimension=1, tiled=True)]
    dot_general x28 -> x0, matrix products: 399 us -> none  [the longest x2 71.3 us: attend_back(): jnp.einsum('hqk,qhd->khd', grad_scores, query_block, preferred_element_ty...]
    unnamed x15 -> x5, waiting for transfers between devices: 303 us -> 90.2 us
    pallas_call x0 -> x9, Pallas kernels: none -> 188 us  [the longest x1 48.5 us: attend_back(): pl.pallas_call(functools.partial(attend_back_kernel, bq=bq, bk=bk), grid_...]
    dynamic_update_slice x8 -> x0, local copies, waits for them, and re-layouts: 119 us -> none  [per_device(): lax.map(attend_back, (queries, keys, values, segments, logsums, grad_atte...]
    reduce_sum x13 -> x3, other arithmetic: 76 us -> 2.79 us  [the longest x2 2.16 us: block_ranges(): high = jnp.sum(segment[None, :] <= last[:, None], axis=1)]
    ppermute x0 -> x39, waiting for transfers between devices: none -> 67.6 us  [the longest x14 46.6 us: swap_dp(): return lax.ppermute(value, 'dp', [(i, i ^ distance) for i in range(count)])]
    psum x3 -> x0, waiting for transfers between devices: 57.9 us -> none  [the longest x1 28.3 us: per_device(): branch = lax.psum(attn_part, 'mp')]
  transfers between devices with their start and end apart: 13 -> 43, of which waited for: 12 -> 23; matrix products, arithmetic and copies ran while one was open for 10% -> 7% of each run, Pallas kernels for 0% -> 10%
where the time goes in v1:
time: 667 us; the launch traced here: 661 us
  waiting for transfers between devices  311 us (47%)
  Pallas kernels  188 us (28%)
  other arithmetic  44.1 us (7%)
  blocking collectives  38.8 us (6%)
  starting transfers between devices  37.5 us (6%)
  between operations  24.6 us (4%)
  local copies, waits for them, and re-layouts  17.1 us (3%)
    unnamed x5, waiting for transfers between devices  90.2 us
    all_gather x1, waiting for transfers between devices, per_device(): wide_near = lax.all_gather(wide_shard, 'dp', axis=0, tiled=True)  82.8 us
    all_gather x1, waiting for transfers between devices, per_device(): near = lax.all_gather(near_shard, 'dp', axis=0, tiled=True)  64.3 us
    pallas_call x1, Pallas kernels, attend_back(): pl.pallas_call(functools.partial(attend_back_kernel, bq=bq, bk=bk), grid_...  48.5 us
    ppermute x14, waiting for transfers between devices, swap_dp(): return lax.ppermute(value, 'dp', [(i, i ^ distance) for i in range(count)])  46.6 us
    pallas_call x4, Pallas kernels, weight_grads(): pl.pallas_call(functools.partial(weight_grad_kernel, plan={'lefts': len(l...  46.4 us
    pallas_call x1, Pallas kernels, middle_stage(): pl.pallas_call(functools.partial(middle_kernel, chunk=768), grid_spec=plt...  42.1 us
    all_gather x1, blocking collectives, per_device(): lax.all_gather(norm_params.astype(BF), 'dp', axis=1, tiled=True).astype(F32)  38.8 us
  transfers between devices with their start and end apart: 43, of which 23 were waited for; matrix products, arithmetic and copies ran while one was open for 7% of the time, Pallas kernels for 10%

profile of v1, /device:TPU:0, one launch (start us, length us, event | category | flops | bytes accessed | tf_op | source)
XLA Modules:
  0.0 661.5 jit_solution(16654333148668020576)
XLA Ops:
  11.9 82.8 %all-gather.9.cloned.1.call-done.w1a_ref.w2a_ref = bf16[768,3072]{1,0:T(8,128)(2,1)} async-done(((bf16[48,3072]{1,0:T(8,128)(2,1)}), bf16[768,3072]{1,0:T(8,128)(2,1)}) %all-gather.9.cloned.1.call-update) | async-done | bytes 4718608 | tf_op jit(solution)/shard_map/all_gather | solution.py:623
  94.6 64.3 %all-gather.7.cloned.1.call-done.wqa_ref.woa_ref = bf16[768,1536]{1,0:T(8,128)(2,1)} async-done(((bf16[48,1536]{1,0:T(8,128)(2,1)}), bf16[768,1536]{1,0:T(8,128)(2,1)}) %all-gather.7.cloned.1.call-update) | async-done | bytes 2359312 | tf_op jit(solution)/shard_map/all_gather | solution.py:621
  165.7 38.8 %all-gather = bf16[16,48,8]{1,2,0:T(8,128)(2,1)S(1)} all-gather(bf16[1,48,8]{1,2,0:T(8,128)(2,1)S(1)} %convert_bitcast_fusion.4), channel_id=1, replica_groups=mesh['dp'=16,'mp'=2] {'dp'}, dimensions={0}, use_global_device_ids=true | all-gather | bytes 13056 | tf_op jit(solution)/shard_map/all_gather | solution.py:620
  210.8 6.6 all-gather.5.cloned.1.call-done.wa_ref
  218.9 10.8 %first_stage.1 = (bf16[1024,768]{1,0:T(8,128)(2,1)}, bf16[1024,768]{1,0:T(8,128)(2,1)}, bf16[1024,768]{1,0:T(8,128)(2,1)}, bf16[1024,768]{1,0:T(8,128)(2,1)}) custom-call(s32[1]{0:T(128)} %bitcast.2.half, bf16[2048,768]{1,0:T(8,128)(2,1)} %x_ref.5, bf16[2048,128]{1,0:T(8,128)(2,1)} %c_ref.5, bf16[4608,128]{1,0:T(8,128)(2,1)} %all-gather.5.cloned.1.call-done.wa_ref, ...), custom_call_target="tpu_custom_call" | custom-call | tf_op jit(solution)/shard_map/first_stage/pallas_call | solution.py:122
  229.7 26.3 %attend.1 = (bf16[1024,768]{1,0:T(8,128)(2,1)}, f32[6,2,1024]{2,1,0:T(2,128)}) custom-call(s32[1]{0:T(128)S(6)} %select_n.225.lo_ref, s32[1]{0:T(128)S(6)} %select_n.226.hi_ref, bf16[1024,768]{1,0:T(8,128)(2,1)} %get-tuple-element.43.q_ref, bf16[1024,768]{1,0:T(8,128)(2,1)} %get-tuple-element.44.k_ref, bf16[1024,768]{1,0:T(8,128)(2,1)} %get-tuple-element.45.v_ref, ...), custom_call_target="tpu_custom_call" | custom-call | tf_op jit(solution)/shard_map/attend/pallas_call | solution.py:214
  256.0 42.1 %middle_stage.1 = (bf16[1024,768]{1,0:T(8,128)(2,1)}, f32[1024,768]{1,0:T(8,128)}, bf16[1024,768]{1,0:T(8,128)(2,1)}, bf16[1024,3072]{1,0:T(8,128)(2,1)}, bf16[1...) custom-call(s32[1]{0:T(128)} %bitcast.2.half, ...), custom_call_target="tpu_custom_call" | custom-call | tf_op jit(solution)/shard_map/middle_stage/pallas_call | solution.py:391
  298.2 48.5 %attend_back.1 = (bf16[1024,768]{1,0:T(8,128)(2,1)}, bf16[1024,768]{1,0:T(8,128)(2,1)}, bf16[1024,768]{1,0:T(8,128)(2,1)}) custom-call(s32[4]{0:T(128)} %get-tuple-element.187.lo_ref, s32[4]{0:T(128)} %get-tuple-element.186.hi_ref, bf16[1024,768]{1,0:T(8,128)(2,1)} %get-tuple-element.43.q_ref, bf16[1024,768]{1,0:T(8,128)(2,1)} %get-tuple-element.44.k_ref, ...), custom_call_target="tpu_custom_call" | custom-call | tf_op jit(solution)/shard_map/attend_back/pallas_call | solution.py:287
  346.7 13.6 %last_stage.1 = (f32[1024,768]{1,0:T(8,128)}, f32[144,1536]{1,0:T(8,128)}, f32[8,768]{1,0:T(8,128)}) custom-call(s32[1]{0:T(128)} %bitcast.2.half, bf16[2048,768]{1,0:T(8,128)(2,1)} %x_ref.5, bf16[2048,128]{1,0:T(8,128)(2,1)} %c_ref.5, f32[1024,768]{1,0:T(8,128)} %get-tuple-element.48.dx_ref, bf16[1024,768]{1,0:T(8,128)(2,1)} %get-tuple-element.51.dq_ref.refs_1_, ...), custom_call_target="tpu_custom_call" | custom-call | tf_op jit(solution)/shard_map/last_stage/pallas_call | solution.py:458
  362.5 15.6 %middle_grads_far.1 = bf16[768,3456]{1,0:T(8,128)(2,1)} custom-call(bf16[1024,768]{1,0:T(8,128)(2,1)} %get-tuple-element.56.refs_0_, bf16[1024,768]{1,0:T(8,128)(2,1)} %get-tuple-element.57.refs_1_, bf16[1024,768]{1,0:T(8,128)(2,1)} %get-tuple-element.58.refs_2_, bf16[1024,3072]{1,0:T(8,128)(2,1)} %get-tuple-element.59.refs_3_, ...), custom_call_target="tpu_custom_call" | custom-call | tf_op jit(solution)/shard_map/middle_grads_far/pallas_call | solution.py:508
  383.3 7.5 %first_grads_far.1 = bf16[768,1152]{1,0:T(8,128)(2,1)} custom-call(bf16[1024,768]{1,0:T(8,128)(2,1)} %get-tuple-element.55.refs_0_, bf16[1024,768]{1,0:T(8,128)(2,1)} %get-tuple-element.51.dq_ref.refs_1_, bf16[1024,768]{1,0:T(8,128)(2,1)} %get-tuple-element.52.dk_ref.refs_2_, bf16[1024,768]{1,0:T(8,128)(2,1)} %get-tuple-element.53.dv_ref.refs_3_), custom_call_target="tpu_custom_call" | custom-call | tf_op jit(solution)/shard_map/first_grads_far/pallas_call | solution.py:508
  400.5 5.1 collective-permute-done.27
  407.5 15.9 %middle_grads_near.1 = bf16[768,3456]{1,0:T(8,128)(2,1)} custom-call(bf16[1024,768]{1,0:T(8,128)(2,1)} %get-tuple-element.56.refs_0_, bf16[1024,768]{1,0:T(8,128)(2,1)} %get-tuple-element.57.refs_1_, bf16[1024,768]{1,0:T(8,128)(2,1)} %get-tuple-element.58.refs_2_, bf16[1024,3072]{1,0:T(8,128)(2,1)} %get-tuple-element.59.refs_3_, ...), custom_call_target="tpu_custom_call" | custom-call | tf_op jit(solution)/shard_map/middle_grads_near/pallas_call | solution.py:508
  423.4 7.5 %first_grads_near.1 = bf16[768,1152]{1,0:T(8,128)(2,1)} custom-call(bf16[1024,768]{1,0:T(8,128)(2,1)} %get-tuple-element.55.refs_0_, bf16[1024,768]{1,0:T(8,128)(2,1)} %get-tuple-element.51.dq_ref.refs_1_, bf16[1024,768]{1,0:T(8,128)(2,1)} %get-tuple-element.52.dk_ref.refs_2_, bf16[1024,768]{1,0:T(8,128)(2,1)} %get-tuple-element.53.dv_ref.refs_3_), custom_call_target="tpu_custom_call" | custom-call | tf_op jit(solution)/shard_map/first_grads_near/pallas_call | solution.py:508
  430.9 90.2 %reduce-scatter.4.cloned.1.call-done = f32[48,8]{1,0:T(8,128)} async-done(((f32[768,8]{1,0:T(8,128)}), f32[48,8]{1,0:T(8,128)}) %reduce-scatter.4.cloned.1.call-update) | async-done | bytes 1552
  533.1 4.4 collective-permute-done.5
  539.2 4.1 collective-permute-done.10
  564.9 12.9 %collective-permute-done.21 = bf16[4,2,48,1664]{3,2,0,1:T(8,128)(2,1)S(1)} collective-permute-done((bf16[4,2,48,1664]{3,2,0,1:T(8,128)(2,1)S(1)}, bf16[4,2,48,1664]{3,2,0,1:T(8,128)(2,1)S(1)}, u32[]{:S(2)}, u32[]{:S(2)}) %collective-permute-start.21) | collective-permute-done | bytes 1277984 | tf_op jit(solution)/shard_map/ppermute | solution.py:534
  579.6 9.2 %collective-permute-done.16 = bf16[4,2,48,1792]{3,2,0,1:T(8,128)(2,1)S(1)} collective-permute-done((bf16[4,2,48,1792]{3,2,0,1:T(8,128)(2,1)S(1)}, bf16[4,2,48,1792]{3,2,0,1:T(8,128)(2,1)S(1)}, u32[]{:S(2)}, u32[]{:S(2)}) %collective-permute-start.16) | collective-permute-done | bytes 1376288 | tf_op jit(solution)/shard_map/ppermute | solution.py:534
  590.8 6.3 collective-permute-done.22
  601.8 4.3 collective-permute-done.23
  606.2 6.5 collective-permute-done.24
  612.7 4.1 collective-permute-start.20
  617.0 5.2 collective-permute-done.19
  (245 shorter events, 104.3 us)
Async XLA Ops:
  7.2 87.4 %all-gather.9.cloned.1.call-start = ((), (), s32[]{:S(2)}) async-start(), calls=%async_computation.3 | async-start | bytes 5013504 | tf_op jit(solution)/shard_map/all_gather | solution.py:623
  10.1 148.9 %all-gather.7.cloned.1.call-start = ((), (), s32[]{:S(2)}) async-start(), calls=%async_computation.2 | async-start | bytes 2506752 | tf_op jit(solution)/shard_map/all_gather | solution.py:621
  11.8 205.5 %all-gather.5.cloned.1.call-start = ((), (), s32[]{:S(2)}) async-start(), calls=%async_computation.1 | async-start | bytes 1253376 | tf_op jit(solution)/shard_map/all_gather | solution.py:619
  94.6 161.4 %collective-permute-start.1 = (bf16[768,3072]{1,0:T(8,128)(2,1)}, bf16[768,3072]{1,0:T(8,128)(2,1)}, u32[]{:S(2)}, u32[]{:S(2)}) collective-permute-start(bf16[768,3072]{1,0:T(8,128)(2,1)} %all-gather.9.cloned.1.call-done.w1a_ref.w2a_ref), channel_id=1, source_target_pairs={{0,1},{1,0},{2,3},{3,2},{4,5},{5,4},{6,7},{7,6},{8,9},{9,8},{10,11... | collective-permute-start | bytes 14155784 | tf_op jit(solution)/shard_map/ppermute | solution.py:529
  159.0 58.4 %collective-permute-start = (bf16[768,1536]{1,0:T(8,128)(2,1)}, bf16[768,1536]{1,0:T(8,128)(2,1)S(1)}, u32[]{:S(2)}, u32[]{:S(2)}) collective-permute-start(bf16[768,1536]{1,0:T(8,128)(2,1)} %all-gather.7.cloned.1.call-done.wqa_ref.woa_ref), channel_id=1, source_target_pairs={{0,1},{1,0},{2,3},{3,2},{4,5},{5,4},{6,7},{7,6},{8,9},{9,8},{10,11... | collective-permute-start | bytes 7077896 | tf_op jit(solution)/shard_map/ppermute | solution.py:529
  159.6 361.4 %reduce-scatter.4.cloned.1.call-start = ((), (), s32[]{:S(2)}) async-start(), calls=%async_computation.4 | async-start | bytes 417792
  378.0 172.0 %collective-permute-start.15 = (bf16[768,3456]{1,0:T(8,128)(2,1)}, bf16[768,3456]{1,0:T(8,128)(2,1)}, u32[]{:S(2)}, u32[]{:S(2)}) collective-permute-start(bf16[768,3456]{1,0:T(8,128)(2,1)} %middle_grads_far.1), channel_id=1, source_target_pairs={{0,1},{1,0},{2,3},{3,2},{4,5},{5,4},{6,7},{7,6},{8,9},{9,8},{10,11... | collective-permute-start | bytes 15925256 | tf_op jit(solution)/shard_map/ppermute | solution.py:529
  382.8 11.1 %collective-permute-start.26 = (bf16[16,144,128]{2,1,0:T(8,128)(2,1)}, bf16[16,144,128]{2,1,0:T(8,128)(2,1)S(1)}, u32[]{:S(2)}, u32[]{:S(2)}) collective-permute-start(bf16[16,144,128]{2,1,0:T(8,128)(2,1)} %get-tuple-element.166), channel_id=1, source_target_pairs={{0,1},{1,0},{2,3},{3,2},{4,5},{5,4},{6,7},{7,6},{8,9},{9,8},{10,11... | collective-permute-start | bytes 1769480 | tf_op jit(solution)/shard_map/ppermute | solution.py:529
  390.8 136.8 %collective-permute-start.4 = (bf16[768,1152]{1,0:T(8,128)(2,1)}, bf16[768,1152]{1,0:T(8,128)(2,1)S(1)}, u32[]{:S(2)}, u32[]{:S(2)}) collective-permute-start(bf16[768,1152]{1,0:T(8,128)(2,1)} %first_grads_far.1), channel_id=1, source_target_pairs={{0,1},{1,0},{2,3},{3,2},{4,5},{5,4},{6,7},{7,6},{8,9},{9,8},{10,11... | collective-permute-start | bytes 5308424 | tf_op jit(solution)/shard_map/ppermute | solution.py:529
  406.6 116.5 %collective-permute-start.28 = (bf16[4,144,128]{2,1,0:T(8,128)(2,1)S(1)}, bf16[4,144,128]{2,1,0:T(8,128)(2,1)S(1)}, u32[]{:S(2)}, u32[]{:S(2)}) collective-permute-start(bf16[4,144,128]{2,1,0:T(8,128)(2,1)S(1)} %fusion.35), channel_id=1, source_target_pairs={{0,2},{2,0},{4,6},{6,4},{8,10},{10,8},{12,14},{14,12},{16,18},{18,... | collective-permute-start | bytes 442376 | tf_op jit(solution)/shard_map/ppermute | solution.py:534
  531.0 12.4 %collective-permute-start.10 = (bf16[4,2,48,640]{3,2,0,1:T(8,128)(2,1)S(1)}, bf16[4,2,48,640]{3,2,0,1:T(8,128)(2,1)S(1)}, u32[]{:S(2)}, u32[]{:S(2)}) collective-permute-start(bf16[4,2,48,640]{3,2,0,1:T(8,128)(2,1)S(1)} %fusion.11), channel_id=1, source_target_pairs={{0,2},{2,0},{4,6},{6,4},{8,10},{10,8},{12,14},{14,12},{16,18},{18,... | collective-permute-start | bytes 1474568 | tf_op jit(solution)/shard_map/ppermute | solution.py:534
  545.5 11.7 %collective-permute-start.7 = (bf16[48,512]{1,0:T(8,128)(2,1)S(1)}, bf16[48,512]{1,0:T(8,128)(2,1)S(1)}, u32[]{:S(2)}, u32[]{:S(2)}) collective-permute-start(bf16[48,512]{1,0:T(8,128)(2,1)S(1)} %get-tuple-element.170), channel_id=1, source_target_pairs={{0,8},{2,10},{4,12},{6,14},{8,16},{10,18},{12,20},{14,22},{16,24},... | collective-permute-start | bytes 147464 | tf_op jit(solution)/shard_map/ppermute | solution.py:539
  546.3 11.4 %collective-permute-start.8 = (bf16[48,512]{1,0:T(8,128)(2,1)S(1)}, bf16[48,512]{1,0:T(8,128)(2,1)S(1)}, u32[]{:S(2)}, u32[]{:S(2)}) collective-permute-start(bf16[48,512]{1,0:T(8,128)(2,1)S(1)} %get-tuple-element.172), channel_id=1, source_target_pairs={{0,16},{2,18},{4,20},{6,22},{8,24},{10,26},{12,28},{14,30},{16,0},... | collective-permute-start | bytes 147464 | tf_op jit(solution)/shard_map/ppermute | solution.py:539
  547.5 11.5 %collective-permute-start.9 = (bf16[48,512]{1,0:T(8,128)(2,1)S(1)}, bf16[48,512]{1,0:T(8,128)(2,1)S(1)}, u32[]{:S(2)}, u32[]{:S(2)}) collective-permute-start(bf16[48,512]{1,0:T(8,128)(2,1)S(1)} %get-tuple-element.171), channel_id=1, source_target_pairs={{0,24},{2,26},{4,28},{6,30},{8,0},{10,2},{12,4},{14,6},{16,8},{18,... | collective-permute-start | bytes 147464 | tf_op jit(solution)/shard_map/ppermute | solution.py:539
  552.4 25.4 %collective-permute-start.21 = (bf16[4,2,48,1664]{3,2,0,1:T(8,128)(2,1)S(1)}, bf16[4,2,48,1664]{3,2,0,1:T(8,128)(2,1)S(1)}, u32[]{:S(2)}, u32[]{:S(2)}) collective-permute-start(bf16[4,2,48,1664]{3,2,0,1:T(8,128)(2,1)S(1)} %fusion.1), channel_id=1, source_target_pairs={{0,4},{2,6},{4,0},{6,2},{8,12},{10,14},{12,8},{14,10},{16,20},{18,... | collective-permute-start | bytes 3833864 | tf_op jit(solution)/shard_map/ppermute | solution.py:534
  555.6 33.2 %collective-permute-start.16 = (bf16[4,2,48,1792]{3,2,0,1:T(8,128)(2,1)S(1)}, bf16[4,2,48,1792]{3,2,0,1:T(8,128)(2,1)S(1)}, u32[]{:S(2)}, u32[]{:S(2)}) collective-permute-start(bf16[4,2,48,1792]{3,2,0,1:T(8,128)(2,1)S(1)} %fusion), channel_id=1, source_target_pairs={{0,2},{2,0},{4,6},{6,4},{8,10},{10,8},{12,14},{14,12},{16,18},{18,... | collective-permute-start | bytes 4128776 | tf_op jit(solution)/shard_map/ppermute | solution.py:534
  563.4 75.4 %collective-permute-start.3 = (f32[1024,768]{1,0:T(8,128)S(1)}, f32[1024,768]{1,0:T(8,128)}, u32[]{:S(2)}, u32[]{:S(2)}) collective-permute-start(f32[1024,768]{1,0:T(8,128)S(1)} %copy-done.2), channel_id=1, source_target_pairs={{0,1},{1,0},{2,3},{3,2},{4,5},{5,4},{6,7},{7,6},{8,9},{9,8},{10,11... | collective-permute-start | bytes 9437192 | tf_op jit(solution)/shard_map/ppermute | solution.py:529
  564.2 67.9 %collective-permute-start.2 = (bf16[1024,768]{1,0:T(8,128)(2,1)}, bf16[1024,768]{1,0:T(8,128)(2,1)}, u32[]{:S(2)}, u32[]{:S(2)}) collective-permute-start(bf16[1024,768]{1,0:T(8,128)(2,1)} %get-tuple-element.47), channel_id=1, source_target_pairs={{0,1},{1,0},{2,3},{3,2},{4,5},{5,4},{6,7},{7,6},{8,9},{9,8},{10,11... | collective-permute-start | bytes 4718600 | tf_op jit(solution)/shard_map/ppermute | solution.py:529
  578.1 18.9 %collective-permute-start.22 = (bf16[4,48,1664]{2,1,0:T(8,128)(2,1)S(1)}, bf16[4,48,1664]{2,1,0:T(8,128)(2,1)S(1)}, u32[]{:S(2)}, u32[]{:S(2)}) collective-permute-start(bf16[4,48,1664]{2,1,0:T(8,128)(2,1)S(1)} %fusion.4), channel_id=1, source_target_pairs={{0,2},{2,0},{4,6},{6,4},{8,10},{10,8},{12,14},{14,12},{16,18},{18,... | collective-permute-start | bytes 1916936 | tf_op jit(solution)/shard_map/ppermute | solution.py:534
  589.2 11.0 %collective-permute-start.17 = (bf16[4,48,1792]{2,1,0:T(8,128)(2,1)S(1)}, bf16[4,48,1792]{2,1,0:T(8,128)(2,1)S(1)}, u32[]{:S(2)}, u32[]{:S(2)}) collective-permute-start(bf16[4,48,1792]{2,1,0:T(8,128)(2,1)S(1)} %fusion.3), channel_id=1, source_target_pairs={{0,4},{2,6},{4,0},{6,2},{8,12},{10,14},{12,8},{14,10},{16,20},{18,... | collective-permute-start | bytes 2064392 | tf_op jit(solution)/shard_map/ppermute | solution.py:534
  597.5 15.2 %collective-permute-start.24 = (bf16[48,1664]{1,0:T(8,128)(2,1)S(1)}, bf16[48,1664]{1,0:T(8,128)(2,1)S(1)}, u32[]{:S(2)}, u32[]{:S(2)}) collective-permute-start(bf16[48,1664]{1,0:T(8,128)(2,1)S(1)} %get-tuple-element.164), channel_id=1, source_target_pairs={{0,16},{2,18},{4,20},{6,22},{8,24},{10,26},{12,28},{14,30},{16,0},... | collective-permute-start | bytes 479240 | tf_op jit(solution)/shard_map/ppermute | solution.py:539
  600.2 12.5 %collective-permute-start.25 = (bf16[48,1664]{1,0:T(8,128)(2,1)S(1)}, bf16[48,1664]{1,0:T(8,128)(2,1)S(1)}, u32[]{:S(2)}, u32[]{:S(2)}) collective-permute-start(bf16[48,1664]{1,0:T(8,128)(2,1)S(1)} %get-tuple-element.163), channel_id=1, source_target_pairs={{0,24},{2,26},{4,28},{6,30},{8,0},{10,2},{12,4},{14,6},{16,8},{18,... | collective-permute-start | bytes 479240 | tf_op jit(solution)/shard_map/ppermute | solution.py:539
  612.7 10.9 %collective-permute-start.20 = (bf16[48,1792]{1,0:T(8,128)(2,1)S(1)}, bf16[48,1792]{1,0:T(8,128)(2,1)S(1)}, u32[]{:S(2)}, u32[]{:S(2)}) collective-permute-start(bf16[48,1792]{1,0:T(8,128)(2,1)S(1)} %get-tuple-element.160), channel_id=1, source_target_pairs={{0,24},{2,26},{4,28},{6,30},{8,0},{10,2},{12,4},{14,6},{16,8},{18,... | collective-permute-start | bytes 516104 | tf_op jit(solution)/shard_map/ppermute | solution.py:539
  616.9 12.2 %collective-permute-start.38 = (f32[144,128]{1,0:T(8,128)S(1)}, f32[144,128]{1,0:T(8,128)}, u32[]{:S(2)}, u32[]{:S(2)}) collective-permute-start(f32[144,128]{1,0:T(8,128)S(1)} %get-tuple-element.151), channel_id=1, source_target_pairs={{0,1},{1,0},{2,3},{3,2},{4,5},{5,4},{6,7},{7,6},{8,9},{9,8},{10,11... | collective-permute-start | bytes 221192 | tf_op jit(solution)/shard_map/ppermute | solution.py:529
  (56 other events, 864.6 us)
Sparse Core Ops, SparseCore 0:
  11.4 83.1 all-gather.8
  98.0 60.9 all-gather.6
  162.3 54.9 all-gather.4
  400.6 120.4 reduce-scatter.3

commit v2 on v1

--- a/solution.py
+++ b/solution.py
@@ -376,10 +376,10 @@
     dp_ref[0:1, :] += jnp.sum(dn * spread, axis=0, keepdims=True)
 
 
-def middle_stage(half, tokens, out_grad, cond, mixed, wa, norms, near, far, wide_near, wide_far):
+def middle_stage(half, tokens, out_grad, cond, mixed, wa, norms, wide_near, wide_far):
     width = tokens.shape[1]
     rows = mixed.shape[0]
-    hidden = wide_near.shape[1] // 2
+    hidden = (wide_near.shape[1] - width // 2) // 2
     blocks = rows // ROW_BLOCK
     mine = lambda i, half: (half[0] * blocks + i, 0)
     plain = lambda i, half: (i, 0)
@@ -400,8 +400,8 @@
                 row,
                 resident(wa.shape, (0, 0)),
                 resident(norms.shape, (0, 0)),
-                resident((width, width // 2), (0, 3)),
-                resident((width, width // 2), (0, 3)),
+                resident((width, width // 2), (0, 4 * hidden // width)),
+                resident((width, width // 2), (0, 4 * hidden // width)),
                 resident((width, hidden), (0, 0)),
                 resident((width, hidden), (0, 0)),
                 resident((width, hidden), (0, 1)),
@@ -416,7 +416,7 @@
                    narrow, shape_of(total, F32), shape_of((8, width), F32)],
         compiler_params=params(),
         name="middle_stage",
-    )(half, tokens, out_grad, cond, mixed, wa, norms, near, far, wide_near, wide_far,
+    )(half, tokens, out_grad, cond, mixed, wa, norms, wide_near, wide_far, wide_near, wide_far,
       wide_near, wide_far)
 
 
@@ -521,6 +521,293 @@
     )(*lefts, *rights)
 
 
+class Gather:
+    def __init__(self, shard, near, far, cut, sems, place):
+        outer, inner, mid, core = place["outer"], place["x"], place["y"], place["core"]
+        z = place["z"]
+        columns = near.shape[-1]
+        split = near.shape[0] != place["outer"] * 4
+        rows = near.shape[0] // (4 * outer)
+
+        def slots(ref, first, number, cols):
+            if split:
+                at = pl.multiple_of(first * rows, 16)
+                return ref.at[pl.ds(at, number * rows), cols]
+            return ref.at[pl.ds(first, number), core, :, cols]
+
+        def copy(src, dst, name, index, device):
+            return pltpu.make_async_remote_copy(
+                src_ref=src,
+                dst_ref=dst,
+                send_sem=sems[name].at[0, index],
+                recv_sem=sems[name].at[1, index],
+                device_id=device,
+                device_id_type=pl.DeviceIdType.MESH,
+            )
+
+        def peer(zz, yy, xx):
+            return (4 * zz + 2 * yy + xx, core)
+
+        whole = slice(None)
+        parts = [("a", slice(0, cut))] + ([("b", slice(cut, columns))] if cut < columns else [])
+        mine = 4 * z + 2 * mid + inner
+        self.outer = outer
+        self.parts = [name for name, _ in parts]
+        self.local = (shard, slots(near, mine, 1, whole))
+        source = shard if split else shard
+        self.hops = {
+            hop: copy(source, slots(near, mine, 1, whole), "hop", hop - 1,
+                      peer(lax.rem(z + hop, outer), mid, inner))
+            for hop in range(1, outer)
+        }
+        self.one, self.two, self.swap = {}, {}, {}
+        for step in range(outer):
+            zz = lax.rem(z + outer - step, outer)
+            base = 4 * zz
+            for index, (name, cols) in enumerate(parts):
+                own = base + 2 * mid + inner
+                device = peer(z, mid, 1 - inner) if name == "a" else peer(z, 1 - mid, inner)
+                if step == 0:
+                    src = shard.at[:, cols] if split else shard.at[:, :, cols]
+                else:
+                    src = slots(near, own, 1, cols)
+                self.one[name, step] = copy(
+                    src, slots(near, own, 1, cols), "one", index * outer + step, device
+                )
+            if True:
+                self.two["a", step] = [
+                    copy(slots(near, base + 2 * mid, 2, parts[0][1]),
+                         slots(near, base + 2 * mid, 2, parts[0][1]),
+                         "two", step, peer(z, 1 - mid, inner))
+                ]
+            if len(parts) > 1:
+                self.two["b", step] = [
+                    copy(slots(near, base + 2 * yy + inner, 1, parts[1][1]),
+                         slots(near, base + 2 * yy + inner, 1, parts[1][1]),
+                         "two", outer + 2 * step + yy, peer(z, mid, 1 - inner))
+                    for yy in range(2)
+                ]
+            target = far if split else near
+            self.swap[step] = copy(
+                slots(near, base, 4, whole), slots(target, base, 4, whole),
+                "swap", step, (4 * z + 2 * mid + inner, 1 - core)
+            )
+
+    @staticmethod
+    def semaphores(outer):
+        kind = pltpu.SemaphoreType.DMA
+        return [kind((2, outer)), kind((2, 2 * outer)), kind((2, 3 * outer)), kind((2, outer))]
+
+    @staticmethod
+    def named(refs):
+        return dict(zip(("hop", "one", "two", "swap"), refs))
+
+    def start_hops(self):
+        for hop in self.hops.values():
+            hop.start()
+
+    def phase_one(self, step):
+        if step:
+            self.hops[step].wait_recv()
+        for name in self.parts:
+            self.one[name, step].start()
+
+    def phase_two(self, step):
+        for name in self.parts:
+            self.one[name, step].wait_recv()
+        for name in self.parts:
+            for entry in self.two[name, step]:
+                entry.start()
+
+    def phase_swap(self, step):
+        for name in self.parts:
+            for entry in self.two[name, step]:
+                entry.wait_recv()
+        self.swap[step].start()
+
+    def finish(self, step):
+        self.swap[step].wait_recv()
+
+    def drain(self):
+        for hop in self.hops.values():
+            hop.wait_send()
+        for step in range(self.outer):
+            for name in self.parts:
+                self.one[name, step].wait_send()
+                for entry in self.two[name, step]:
+                    entry.wait_send()
+            self.swap[step].wait_send()
+
+
+def my_place(count):
+    me, core = lax.axis_index("dp"), lax.axis_index("mp")
+    return {"outer": count // 4, "z": me // 4, "y": lax.rem(me // 2, 2), "x": lax.rem(me, 2),
+            "core": core, "me": me}
+
+
+def meet(place):
+    z, y, x, core, outer = (place[name] for name in ("z", "y", "x", "core", "outer"))
+    here = 2 * y + x
+    others = [(4 * lax.rem(z + hop, outer) + here, core) for hop in range(1, outer)]
+    others += [(4 * z + 2 * y + 1 - x, core), (4 * z + 2 * (1 - y) + x, core),
+               (4 * z + here, 1 - core)]
+    barrier = pltpu.get_barrier_semaphore()
+    for other in others:
+        pl.semaphore_signal(barrier, inc=1, device_id=other, device_id_type=pl.DeviceIdType.MESH)
+    pl.semaphore_wait(barrier, len(others))
+
+
+def opening_kernel(tok_ref, cond_ref, g1_ref, ada_ref, g2_ref, cos_ref, sin_ref, fq_ref, fk_ref,
+                   h_ref, q_ref, k_ref, v_ref, o_ref, lse_ref, near_ref, far_ref, wa_ref,
+                   norm_ref, wide_near, wide_far,
+                   x_vm, c_vm, qz, kz, vt, local, *sems, count, cuts, bk):
+    place = my_place(count)
+    outer, core = place["outer"], place["core"]
+    rows, width = x_vm.shape
+    own = width // 2
+    groups = [Gather.named(sems[4 * i : 4 * i + 4]) for i in range(3)]
+    small = Gather(g1_ref, near_ref, far_ref, cuts[0], groups[0], place)
+    ada = Gather(ada_ref, wa_ref, None, ada_ref.shape[-1], groups[1], place)
+    wide = Gather(g2_ref, wide_near, wide_far, cuts[1], groups[2], place)
+
+    start = pl.multiple_of(core * rows, rows)
+    loads = [
+        pltpu.make_async_copy(tok_ref.at[pl.ds(start, rows)], x_vm, local.at[0]),
+        pltpu.make_async_copy(cond_ref.at[pl.ds(start, rows)], c_vm, local.at[1]),
+        pltpu.make_async_copy(*wide.local, local.at[2]),
+        pltpu.make_async_copy(*small.local, local.at[3]),
+        pltpu.make_async_copy(*ada.local, local.at[4]),
+    ]
+    for load in loads:
+        load.start()
+    meet(place)
+    ada.start_hops()
+    small.start_hops()
+    for load in loads:
+        load.wait()
+    for step in range(outer):
+        ada.phase_one(step)
+        small.phase_one(step)
+    wide.start_hops()
+    for step in range(outer):
+        ada.phase_two(step)
+        small.phase_two(step)
+    for step in range(outer):
+        ada.phase_swap(step)
+        small.phase_swap(step)
+    wide.phase_one(0)
+    for step in range(outer):
+        ada.finish(step)
+        small.finish(step)
+
+    table = near_ref[:, 3 * own :].astype(F32).T
+    norm_ref[...] = table[0:8, :]
+    wa = wa_ref[...].reshape(6 * width, c_vm.shape[1])
+
+    def row_block(i, _):
+        at = pl.ds(pl.multiple_of(i * ROW_BLOCK, ROW_BLOCK), ROW_BLOCK)
+        cond = silu_low(c_vm[at, :])
+        shift = dot(cond, wa[:width], NT) + norm_ref[2:3, :]
+        scale = dot(cond, wa[width : 2 * width], NT) + norm_ref[3:4, :]
+        normal, _ = normalize(x_vm[at, :].astype(F32))
+        h = (normal * norm_ref[0:1, :] * (1.0 + scale) + shift).astype(BF)
+        h_ref[at, :] = h
+        cos = jnp.concatenate([cos_ref[at, :]] * (own // LANES), axis=1)
+        sin = jnp.concatenate([sin_ref[at, :]] * (own // LANES), axis=1)
+        for first, w_ref in ((0, near_ref), (own, far_ref)):
+            cols = slice(first, first + own)
+            query = dot(h, w_ref[:, 0:own])
+            query = query * cos + swap_halves(query) * sin
+            q_ref[at, cols] = (query * HEAD_DIM**-0.5).astype(BF)
+            key = dot(h, w_ref[:, own : 2 * own])
+            k_ref[at, cols] = (key * cos + swap_halves(key) * sin).astype(BF)
+            v_ref[at, cols] = dot(h, w_ref[:, 2 * own : 3 * own]).astype(BF)
+        for step in range(1, outer):
+
+            @pl.when(i == step - 1)
+            def _():
+                wide.phase_one(step)
+
+        return 0
+
+    lax.fori_loop(0, rows // ROW_BLOCK, row_block, 0)
+
+    def head_pair(p, _):
+        lanes = pl.ds(pl.multiple_of(p * LANES, LANES), LANES)
+        qz[0], qz[1] = split_heads(q_ref[:, lanes], fq_ref[...])
+        kz[0], kz[1] = split_heads(k_ref[:, lanes], fk_ref[...])
+        vt[...] = v_ref[:, lanes].T
+        state = [None, None]
+        for j in range(rows // bk):
+            block = slice(j * bk, (j + 1) * bk)
+            scores = [dot(kz[h, block, :], qz[h], NT) for h in range(2)]
+            for h in range(2):
+                values = vt[HEAD_DIM * h : HEAD_DIM * (h + 1), block]
+                top = jnp.max(scores[h], axis=0, keepdims=True)
+                if j:
+                    top = jnp.maximum(state[h][0], top)
+                weights = jnp.exp(scores[h] - top)
+                total = jnp.sum(weights, axis=0, keepdims=True)
+                result = dot(values, weights.astype(BF))
+                if j:
+                    fade = jnp.exp(state[h][0] - top)
+                    total = state[h][1] * fade + total
+                    result = state[h][2] * fade + result
+                state[h] = (top, total, result)
+        done = jnp.concatenate([entry[2] / entry[1] for entry in state], axis=0)
+        o_ref[:, lanes] = done.T.astype(BF)
+        for h in range(2):
+            lse_ref[p, h : h + 1, :] = state[h][0] + jnp.log(state[h][1])
+
+        for step in range(outer):
+
+            @pl.when(p == step // 2)
+            def _():
+                wide.phase_two(step)
+
+            @pl.when(p == 3 + step // 2)
+            def _():
+                wide.phase_swap(step)
+
+        return 0
+
+    lax.fori_loop(0, width // LANES, head_pair, 0)
+    for step in range(outer):
+        wide.finish(step)
+    for group in (ada, small, wide):
+        group.drain()
+
+
+def opening(count, tokens, cond, small_shard, ada_shard, wide_shard, tables, features):
+    rows, width = tokens.shape[0] // 2, tokens.shape[1]
+    conds = cond.shape[1]
+    vm = pl.BlockSpec(memory_space=pltpu.VMEM)
+    hbm = pl.BlockSpec(memory_space=pl.ANY)
+    small = shape_of((width, small_shard.shape[1]), BF)
+    wide = shape_of((width, wide_shard.shape[1]), BF)
+    act = shape_of((rows, width), BF)
+    pairs = width // LANES
+    scratch = pltpu.VMEM((2, rows, LANES), BF)
+    cuts = (512, wide_shard.shape[1] // 2 // LANES * LANES)
+    return pl.pallas_call(
+        functools.partial(opening_kernel, count=count, cuts=cuts, bk=512),
+        in_specs=[hbm, hbm] + [vm] * 7,
+        out_specs=[vm] * 10 + [hbm, hbm],
+        out_shape=[act, act, act, act, act, shape_of((pairs, 2, rows), F32), small, small,
+                   shape_of((count, 2, ada_shard.shape[1], conds), BF),
+                   shape_of((8, width), F32), wide, wide],
+        scratch_shapes=[
+            pltpu.VMEM((rows, width), BF), pltpu.VMEM((rows, conds), BF),
+            scratch, scratch, pltpu.VMEM((LANES, rows), BF),
+            pltpu.SemaphoreType.DMA((5,)),
+        ] + Gather.semaphores(count // 4) * 3,
+        compiler_params=pltpu.CompilerParams(
+            vmem_limit_bytes=VMEM_LIMIT, collective_id=0, has_side_effects=True
+        ),
+        name="opening",
+    )(tokens, cond, small_shard, ada_shard, wide_shard, *tables, *features)
+
+
 def factors(count):
     return (count // 4, 2, 2)
 
@@ -612,27 +899,40 @@
     half_ref = half.reshape(1).astype(jnp.int32)
     token_total = float(tokens.shape[0] * count)
 
-    ada_shard = ada_weight.T.astype(BF)
-    qkv_shard = qkv_weight.astype(BF).transpose(1, 0, 2).reshape(part, -1)
-    near_shard = jnp.concatenate([qkv_shard, out_weight.astype(BF).T], axis=1)
-    wide_shard = jnp.concatenate([up_weight.astype(BF), down_weight.astype(BF).T], axis=1)
-    wa = lax.all_gather(ada_shard, "dp", axis=0, tiled=True)
-    norms = lax.all_gather(norm_params.astype(BF), "dp", axis=1, tiled=True).astype(F32)
-    near = lax.all_gather(near_shard, "dp", axis=0, tiled=True)
-    far = swap_mp(near)
-    wide_near = lax.all_gather(wide_shard, "dp", axis=0, tiled=True)
-    wide_far = swap_mp(wide_near)
-
+    ada_shard = ada_weight.T.astype(BF).reshape(2, -1, cond.shape[1])
+    small_shard = jnp.concatenate(
+        [
+            qkv_weight.astype(BF).transpose(1, 0, 2).reshape(part, -1),
+            jnp.pad(norm_params.astype(BF).T, ((0, 0), (0, LANES - 8))),
+        ],
+        axis=1,
+    )
+    wide_shard = jnp.concatenate(
+        [up_weight.astype(BF), down_weight.astype(BF).T, out_weight.astype(BF).T], axis=1
+    )
     segment = pick(segments, half, 0)
     features = document_features(segment)
     tables = rope_tables(rows)
-
-    h_one, queries, keys, values = first_stage(
-        half_ref, tokens, cond, wa, norms, near, far, tables
-    )
-    mixed, lse = attend(queries, keys, values, segment, features)
+    if part % 16 == 0 and ada_shard.shape[1] % 16 == 0:
+        (h_one, queries, keys, values, mixed, lse, near, far, wa, norms, wide_near,
+         wide_far) = opening(
+            count, tokens, cond, small_shard, pick(ada_shard, half, 0)[None], wide_shard, tables,
+            features,
+        )
+        wa = wa.reshape(-1, conds)
+    else:
+        wa = lax.all_gather(ada_shard.reshape(-1, conds), "dp", axis=0, tiled=True)
+        near = lax.all_gather(small_shard, "dp", axis=0, tiled=True)
+        far = swap_mp(near)
+        norms = near[:, -LANES:].T[:8].astype(F32)
+        wide_near = lax.all_gather(wide_shard, "dp", axis=0, tiled=True)
+        wide_far = swap_mp(wide_near)
+        h_one, queries, keys, values = first_stage(
+            half_ref, tokens, cond, wa, norms, near, far, tables
+        )
+        mixed, lse = attend(queries, keys, values, segment, features)
     result, dx, upstream, z, gy, h_two, du, ga, dwa_two, dp_two = middle_stage(
-        half_ref, tokens, out_grad, cond, mixed, wa, norms, near, far, wide_near, wide_far
+        half_ref, tokens, out_grad, cond, mixed, wa, norms, wide_near, wide_far
     )
     result_far = swap_mp(result)
 
@@ -669,14 +969,15 @@
     dwa = jnp.concatenate([dwa_one, dwa_two], axis=1)
     ada_cols = dwa.shape[1] // count
     dwa_rows = dwa[:conds].T.astype(BF).reshape(count, 2, ada_cols // 2, conds)
-    ada_near, ada_far = pick(dwa_rows, half, 1), swap_mp(pick(dwa_rows, 1 - half, 1))
-    ada_half = scatter_sum([ada_near, ada_far], (2, 1))
     norm_rows = jnp.concatenate(
         [dp_one[0:1], dp_two[0:1], dwa[conds].reshape(6, width)], axis=0
-    )
-    norm_sum = lax.psum_scatter(
-        norm_rows + swap_mp(norm_rows), "dp", scatter_dimension=1, tiled=True
-    )
+    ).astype(BF)
+    norm_rows = norm_rows.reshape(8, count, part).transpose(1, 0, 2)
+    norm_rows = jnp.pad(norm_rows, ((0, 0), (0, 0), (0, conds - part)))
+    ada_near = jnp.concatenate([pick(dwa_rows, half, 1), norm_rows], axis=1)
+    ada_far = swap_mp(jnp.concatenate([pick(dwa_rows, 1 - half, 1), norm_rows], axis=1))
+    ada_sum = scatter_sum([ada_near, ada_far], (2, 1))
+    ada_half, norm_sum = ada_sum[: ada_cols // 2], ada_sum[ada_cols // 2 :, :part]
 
     wide_cols = du.shape[1] // 2
     up_mean = middle_sum[:, :wide_cols] / token_total

time: 667 us -> 429 us (0.64)
  waiting for transfers between devices: 311 us -> 81.9 us
  Pallas kernels: 188 us -> 246 us
  blocking collectives: 38.8 us -> 0 us
  between operations: 24.6 us -> 8.74 us
  local copies, waits for them, and re-layouts: 17.1 us -> 7.53 us
    all_gather x3 -> x0, waiting for transfers between devices: 154 us -> none  [the longest x1 82.8 us: per_device(): wide_near = lax.all_gather(wide_shard, 'dp', axis=0, tiled=True)]
    unnamed x5 -> x0, waiting for transfers between devices: 90.2 us -> none
    pallas_call x2 -> x1, Pallas kernels: 37.2 us -> 94.4 us  [opening(): pl.pallas_call(functools.partial(opening_kernel, count=count, cuts=cuts,...]
    all_gather x1 -> x0, blocking collectives: 38.8 us -> none  [per_device(): lax.all_gather(norm_params.astype(BF), 'dp', axis=1, tiled=True).astype(F32)]
    ppermute x14, waiting for transfers between devices: 46.6 us -> 57.8 us  [swap_dp(): return lax.ppermute(value, 'dp', [(i, i ^ distance) for i in range(count)])]
  transfers between devices with their start and end apart: 43 -> 36, of which waited for: 23 -> 18; matrix products, arithmetic and copies ran while one was open for 7% -> 8% of each run, Pallas kernels for 10% -> 22%
where the time goes in v2:
time: 429 us; the launch traced here: 421 us
  Pallas kernels  246 us (57%)
  waiting for transfers between devices  81.9 us (19%)
  other arithmetic  41 us (10%)
  starting transfers between devices  35.8 us (8%)
  between operations  8.74 us (2%)
  local copies, waits for them, and re-layouts  7.53 us (2%)
    pallas_call x1, Pallas kernels, opening(): pl.pallas_call(functools.partial(opening_kernel, count=count, cuts=cuts,...  94.4 us
    ppermute x14, waiting for transfers between devices, swap_dp(): return lax.ppermute(value, 'dp', [(i, i ^ distance) for i in range(count)])  57.8 us
    pallas_call x1, Pallas kernels, attend_back(): pl.pallas_call(functools.partial(attend_back_kernel, bq=bq, bk=bk), grid_...  49.6 us
    pallas_call x4, Pallas kernels, weight_grads(): pl.pallas_call(functools.partial(weight_grad_kernel, plan={'lefts': len(l...  46.3 us
    pallas_call x1, Pallas kernels, middle_stage(): pl.pallas_call(functools.partial(middle_kernel, chunk=768), grid_spec=plt...  42.3 us
    ppermute x15, starting transfers between devices, turn_dp(): lax.ppermute(value, 'dp', [(i, (i + distance) % count) for i in range(cou...  24.7 us
    ppermute x15, waiting for transfers between devices, turn_dp(): lax.ppermute(value, 'dp', [(i, (i + distance) % count) for i in range(cou...  21.7 us
    pallas_call x1, Pallas kernels, last_stage(): pl.pallas_call(last_kernel, grid_spec=pltpu.PrefetchScalarGridSpec(num_sc...  13.7 us
  transfers between devices with their start and end apart: 36, of which 18 were waited for; matrix products, arithmetic and copies ran while one was open for 8% of the time, Pallas kernels for 22%

profile of v2, /device:TPU:0, one launch (start us, length us, event | category | flops | bytes accessed | tf_op | source)
XLA Modules:
  0.0 421.2 jit_solution(240909786609044385)
XLA Ops:
  8.9 94.4 %opening.1 = (bf16[1024,768]{1,0:T(8,128)(2,1)}, bf16[1024,768]{1,0:T(8,128)(2,1)}, bf16[1024,768]{1,0:T(8,128)(2,1)}, bf16[1024,768]{1,0:T(8,128)(2,1)}, bf16[1...) custom-call(bf16[2048,768]{1,0:T(8,128)(2,1)} %x_ref.3, ...), custom_call_target="tpu_custom_call" | custom-call | tf_op jit(solution)/shard_map/opening/pallas_call | solution.py:792
  103.3 42.3 %middle_stage.1 = (bf16[1024,768]{1,0:T(8,128)(2,1)}, f32[1024,768]{1,0:T(8,128)}, bf16[1024,768]{1,0:T(8,128)(2,1)}, bf16[1024,3072]{1,0:T(8,128)(2,1)}, bf16[1...) custom-call(s32[1]{0:T(128)} %bitcast.half, ...), custom_call_target="tpu_custom_call" | custom-call | tf_op jit(solution)/shard_map/middle_stage/pallas_call | solution.py:391
  145.6 15.6 %middle_grads_far.1 = bf16[768,3456]{1,0:T(8,128)(2,1)} custom-call(bf16[1024,768]{1,0:T(8,128)(2,1)} %get-tuple-element.68.refs_0_, bf16[1024,768]{1,0:T(8,128)(2,1)} %get-tuple-element.69.refs_1_, bf16[1024,768]{1,0:T(8,128)(2,1)} %get-tuple-element.70.refs_2_, bf16[1024,3072]{1,0:T(8,128)(2,1)} %get-tuple-element.71.refs_3_, ...), custom_call_target="tpu_custom_call" | custom-call | tf_op jit(solution)/shard_map/middle_grads_far/pallas_call | solution.py:508
  162.6 49.6 %attend_back.1 = (bf16[1024,768]{1,0:T(8,128)(2,1)}, bf16[1024,768]{1,0:T(8,128)(2,1)}, bf16[1024,768]{1,0:T(8,128)(2,1)}) custom-call(s32[4]{0:T(128)} %get-tuple-element.172.lo_ref, s32[4]{0:T(128)} %get-tuple-element.171.hi_ref, bf16[1024,768]{1,0:T(8,128)(2,1)} %get-tuple-element.56.q_ref, bf16[1024,768]{1,0:T(8,128)(2,1)} %get-tuple-element.57.k_ref, ...), custom_call_target="tpu_custom_call" | custom-call | tf_op jit(solution)/shard_map/attend_back/pallas_call | solution.py:287
  212.2 13.7 %last_stage.1 = (f32[1024,768]{1,0:T(8,128)}, f32[144,1536]{1,0:T(8,128)}, f32[8,768]{1,0:T(8,128)}) custom-call(s32[1]{0:T(128)} %bitcast.half, bf16[2048,768]{1,0:T(8,128)(2,1)} %x_ref.3, bf16[2048,128]{1,0:T(8,128)(2,1)} %c_ref.3, f32[1024,768]{1,0:T(8,128)} %get-tuple-element.55.dx_ref, bf16[1024,768]{1,0:T(8,128)(2,1)} %get-tuple-element.61.dq_ref.refs_1_, ...), custom_call_target="tpu_custom_call" | custom-call | tf_op jit(solution)/shard_map/last_stage/pallas_call | solution.py:458
  234.9 7.5 %first_grads_far.1 = bf16[768,1152]{1,0:T(8,128)(2,1)} custom-call(bf16[1024,768]{1,0:T(8,128)(2,1)} %get-tuple-element.67.refs_0_, bf16[1024,768]{1,0:T(8,128)(2,1)} %get-tuple-element.61.dq_ref.refs_1_, bf16[1024,768]{1,0:T(8,128)(2,1)} %get-tuple-element.62.dk_ref.refs_2_, bf16[1024,768]{1,0:T(8,128)(2,1)} %get-tuple-element.63.dv_ref.refs_3_), custom_call_target="tpu_custom_call" | custom-call | tf_op jit(solution)/shard_map/first_grads_far/pallas_call | solution.py:508
  244.5 5.1 %collective-permute-done.26 = bf16[4,152,128]{2,1,0:T(8,128)(2,1)S(1)} collective-permute-done((bf16[4,152,128]{2,1,0:T(8,128)(2,1)S(1)}, bf16[4,152,128]{2,1,0:T(8,128)(2,1)S(1)}, u32[]{:S(2)}, u32[]{:S(2)}) %collective-permute-start.26) | collective-permute-done | bytes 155680 | tf_op jit(solution)/shard_map/ppermute | solution.py:821
  249.7 2.5 collective-permute-start.27
  252.2 4.5 %collective-permute-start.28 = (bf16[152,128]{1,0:T(8,128)(2,1)S(1)}, bf16[152,128]{1,0:T(8,128)(2,1)S(1)}, u32[]{:S(2)}, u32[]{:S(2)}) collective-permute-start(bf16[152,128]{1,0:T(8,128)(2,1)S(1)} %get-tuple-element.162), channel_id=1, source_target_pairs={{0,16},{2,18},{4,20},{6,22},{8,24},{10,26},{12,28},{14,30},{16,0},... | collective-permute-start | bytes 116744 | tf_op jit(solution)/shard_map/ppermute | solution.py:826
  256.7 15.8 %middle_grads_near.1 = bf16[768,3456]{1,0:T(8,128)(2,1)} custom-call(bf16[1024,768]{1,0:T(8,128)(2,1)} %get-tuple-element.68.refs_0_, bf16[1024,768]{1,0:T(8,128)(2,1)} %get-tuple-element.69.refs_1_, bf16[1024,768]{1,0:T(8,128)(2,1)} %get-tuple-element.70.refs_2_, bf16[1024,3072]{1,0:T(8,128)(2,1)} %get-tuple-element.71.refs_3_, ...), custom_call_target="tpu_custom_call" | custom-call | tf_op jit(solution)/shard_map/middle_grads_near/pallas_call | solution.py:508
  272.5 7.5 %first_grads_near.1 = bf16[768,1152]{1,0:T(8,128)(2,1)} custom-call(bf16[1024,768]{1,0:T(8,128)(2,1)} %get-tuple-element.67.refs_0_, bf16[1024,768]{1,0:T(8,128)(2,1)} %get-tuple-element.61.dq_ref.refs_1_, bf16[1024,768]{1,0:T(8,128)(2,1)} %get-tuple-element.62.dk_ref.refs_2_, bf16[1024,768]{1,0:T(8,128)(2,1)} %get-tuple-element.63.dv_ref.refs_3_), custom_call_target="tpu_custom_call" | custom-call | tf_op jit(solution)/shard_map/first_grads_near/pallas_call | solution.py:508
  287.3 7.5 %collective-permute-done.3 = bf16[4,2,48,512]{3,2,0,1:T(8,128)(2,1)S(1)} collective-permute-done((bf16[4,2,48,512]{3,2,0,1:T(8,128)(2,1)S(1)}, bf16[4,2,48,512]{3,2,0,1:T(8,128)(2,1)S(1)}, u32[]{:S(2)}, u32[]{:S(2)}) %collective-permute-start.3) | collective-permute-done | bytes 393248 | tf_op jit(solution)/shard_map/ppermute | solution.py:821
  295.3 4.5 %collective-permute-done.8 = bf16[4,2,48,640]{3,2,0,1:T(8,128)(2,1)S(1)} collective-permute-done((bf16[4,2,48,640]{3,2,0,1:T(8,128)(2,1)S(1)}, bf16[4,2,48,640]{3,2,0,1:T(8,128)(2,1)S(1)}, u32[]{:S(2)}, u32[]{:S(2)}) %collective-permute-start.8) | collective-permute-done | bytes 491552 | tf_op jit(solution)/shard_map/ppermute | solution.py:821
  305.4 2.4 collective-permute-start.7
  322.7 16.7 %collective-permute-done.19 = bf16[4,2,48,1664]{3,2,0,1:T(8,128)(2,1)S(1)} collective-permute-done((bf16[4,2,48,1664]{3,2,0,1:T(8,128)(2,1)S(1)}, bf16[4,2,48,1664]{3,2,0,1:T(8,128)(2,1)S(1)}, u32[]{:S(2)}, u32[]{:S(2)}) %collective-permute-start.19) | collective-permute-done | bytes 1277984 | tf_op jit(solution)/shard_map/ppermute | solution.py:821
  340.1 7.6 %collective-permute-done.14 = bf16[4,2,48,1792]{3,2,0,1:T(8,128)(2,1)S(1)} collective-permute-done((bf16[4,2,48,1792]{3,2,0,1:T(8,128)(2,1)S(1)}, bf16[4,2,48,1792]{3,2,0,1:T(8,128)(2,1)S(1)}, u32[]{:S(2)}, u32[]{:S(2)}) %collective-permute-start.14) | collective-permute-done | bytes 1376288 | tf_op jit(solution)/shard_map/ppermute | solution.py:821
  348.8 10.0 %collective-permute-done.20 = bf16[4,48,1664]{2,1,0:T(8,128)(2,1)S(1)} collective-permute-done((bf16[4,48,1664]{2,1,0:T(8,128)(2,1)S(1)}, bf16[4,48,1664]{2,1,0:T(8,128)(2,1)S(1)}, u32[]{:S(2)}, u32[]{:S(2)}) %collective-permute-start.20) | collective-permute-done | bytes 639008 | tf_op jit(solution)/shard_map/ppermute | solution.py:821
  363.3 4.7 %collective-permute-done.21 = bf16[48,1664]{1,0:T(8,128)(2,1)S(1)} collective-permute-done((bf16[48,1664]{1,0:T(8,128)(2,1)S(1)}, bf16[48,1664]{1,0:T(8,128)(2,1)S(1)}, u32[]{:S(2)}, u32[]{:S(2)}) %collective-permute-start.21) | collective-permute-done | bytes 159776 | tf_op jit(solution)/shard_map/ppermute | solution.py:826
  369.0 8.1 %collective-permute-done.22 = bf16[48,1664]{1,0:T(8,128)(2,1)S(1)} collective-permute-done((bf16[48,1664]{1,0:T(8,128)(2,1)S(1)}, bf16[48,1664]{1,0:T(8,128)(2,1)S(1)}, u32[]{:S(2)}, u32[]{:S(2)}) %collective-permute-start.22) | collective-permute-done | bytes 159776 | tf_op jit(solution)/shard_map/ppermute | solution.py:826
  377.1 3.7 collective-permute-start.18
  380.9 6.1 %collective-permute-done.17 = bf16[48,1792]{1,0:T(8,128)(2,1)S(1)} collective-permute-done((bf16[48,1792]{1,0:T(8,128)(2,1)S(1)}, bf16[48,1792]{1,0:T(8,128)(2,1)S(1)}, u32[]{:S(2)}, u32[]{:S(2)}) %collective-permute-start.17) | collective-permute-done | bytes 172064 | tf_op jit(solution)/shard_map/ppermute | solution.py:826
  402.5 2.4 collective-permute-start.33
  404.9 2.4 broadcast_select_fusion.1
  408.4 3.1 pad_maximum_fusion
  (228 shorter events, 74.9 us)
Async XLA Ops:
  161.2 146.8 %collective-permute-start.13 = (bf16[768,3456]{1,0:T(8,128)(2,1)}, bf16[768,3456]{1,0:T(8,128)(2,1)}, u32[]{:S(2)}, u32[]{:S(2)}) collective-permute-start(bf16[768,3456]{1,0:T(8,128)(2,1)} %middle_grads_far.1), channel_id=1, source_target_pairs={{0,1},{1,0},{2,3},{3,2},{4,5},{5,4},{6,7},{7,6},{8,9},{9,8},{10,11... | collective-permute-start | bytes 15925256 | tf_op jit(solution)/shard_map/ppermute | solution.py:816
  234.8 9.5 %collective-permute-start.25 = (bf16[4,2,152,128]{3,2,1,0:T(8,128)(2,1)S(1)}, bf16[4,2,152,128]{3,2,1,0:T(8,128)(2,1)S(1)}, u32[]{:S(2)}, u32[]{:S(2)}) collective-permute-start(bf16[4,2,152,128]{3,2,1,0:T(8,128)(2,1)S(1)} %fusion.16), channel_id=1, source_target_pairs={{0,4},{2,6},{4,0},{6,2},{8,12},{10,14},{12,8},{14,10},{16,20},{18,... | collective-permute-start | bytes 933896 | tf_op jit(solution)/shard_map/ppermute | solution.py:821
  242.3 39.0 %collective-permute-start.2 = (bf16[768,1152]{1,0:T(8,128)(2,1)}, bf16[768,1152]{1,0:T(8,128)(2,1)}, u32[]{:S(2)}, u32[]{:S(2)}) collective-permute-start(bf16[768,1152]{1,0:T(8,128)(2,1)} %first_grads_far.1), channel_id=1, source_target_pairs={{0,1},{1,0},{2,3},{3,2},{4,5},{5,4},{6,7},{7,6},{8,9},{9,8},{10,11... | collective-permute-start | bytes 5308424 | tf_op jit(solution)/shard_map/ppermute | solution.py:816
  249.7 30.2 %collective-permute-start.27 = (bf16[152,128]{1,0:T(8,128)(2,1)S(1)}, bf16[152,128]{1,0:T(8,128)(2,1)S(1)}, u32[]{:S(2)}, u32[]{:S(2)}) collective-permute-start(bf16[152,128]{1,0:T(8,128)(2,1)S(1)} %get-tuple-element.160), channel_id=1, source_target_pairs={{0,8},{2,10},{4,12},{6,14},{8,16},{10,18},{12,20},{14,22},{16,24},... | collective-permute-start | bytes 116744 | tf_op jit(solution)/shard_map/ppermute | solution.py:826
  252.2 27.8 %collective-permute-start.28 = (bf16[152,128]{1,0:T(8,128)(2,1)S(1)}, bf16[152,128]{1,0:T(8,128)(2,1)S(1)}, u32[]{:S(2)}, u32[]{:S(2)}) collective-permute-start(bf16[152,128]{1,0:T(8,128)(2,1)S(1)} %get-tuple-element.162), channel_id=1, source_target_pairs={{0,16},{2,18},{4,20},{6,22},{8,24},{10,26},{12,28},{14,30},{16,0},... | collective-permute-start | bytes 116744 | tf_op jit(solution)/shard_map/ppermute | solution.py:826
  256.7 23.2 %collective-permute-start.29 = (bf16[152,128]{1,0:T(8,128)(2,1)S(1)}, bf16[152,128]{1,0:T(8,128)(2,1)S(1)}, u32[]{:S(2)}, u32[]{:S(2)}) collective-permute-start(bf16[152,128]{1,0:T(8,128)(2,1)S(1)} %get-tuple-element.161), channel_id=1, source_target_pairs={{0,24},{2,26},{4,28},{6,30},{8,0},{10,2},{12,4},{14,6},{16,8},{18,... | collective-permute-start | bytes 116744 | tf_op jit(solution)/shard_map/ppermute | solution.py:826
  283.2 11.6 %collective-permute-start.3 = (bf16[4,2,48,512]{3,2,0,1:T(8,128)(2,1)S(1)}, bf16[4,2,48,512]{3,2,0,1:T(8,128)(2,1)S(1)}, u32[]{:S(2)}, u32[]{:S(2)}) collective-permute-start(bf16[4,2,48,512]{3,2,0,1:T(8,128)(2,1)S(1)} %fusion.11), channel_id=1, source_target_pairs={{0,4},{2,6},{4,0},{6,2},{8,12},{10,14},{12,8},{14,10},{16,20},{18,... | collective-permute-start | bytes 1179656 | tf_op jit(solution)/shard_map/ppermute | solution.py:821
  285.6 14.1 %collective-permute-start.8 = (bf16[4,2,48,640]{3,2,0,1:T(8,128)(2,1)S(1)}, bf16[4,2,48,640]{3,2,0,1:T(8,128)(2,1)S(1)}, u32[]{:S(2)}, u32[]{:S(2)}) collective-permute-start(bf16[4,2,48,640]{3,2,0,1:T(8,128)(2,1)S(1)} %fusion.10), channel_id=1, source_target_pairs={{0,2},{2,0},{4,6},{6,4},{8,10},{10,8},{12,14},{14,12},{16,18},{18,... | collective-permute-start | bytes 1474568 | tf_op jit(solution)/shard_map/ppermute | solution.py:821
  294.9 8.3 %collective-permute-start.4 = (bf16[4,48,512]{2,1,0:T(8,128)(2,1)S(1)}, bf16[4,48,512]{2,1,0:T(8,128)(2,1)S(1)}, u32[]{:S(2)}, u32[]{:S(2)}) collective-permute-start(bf16[4,48,512]{2,1,0:T(8,128)(2,1)S(1)} %fusion.26), channel_id=1, source_target_pairs={{0,2},{2,0},{4,6},{6,4},{8,10},{10,8},{12,14},{14,12},{16,18},{18,... | collective-permute-start | bytes 589832 | tf_op jit(solution)/shard_map/ppermute | solution.py:821
  303.4 11.4 %collective-permute-start.5 = (bf16[48,512]{1,0:T(8,128)(2,1)S(1)}, bf16[48,512]{1,0:T(8,128)(2,1)S(1)}, u32[]{:S(2)}, u32[]{:S(2)}) collective-permute-start(bf16[48,512]{1,0:T(8,128)(2,1)S(1)} %get-tuple-element.156), channel_id=1, source_target_pairs={{0,8},{2,10},{4,12},{6,14},{8,16},{10,18},{12,20},{14,22},{16,24},... | collective-permute-start | bytes 147464 | tf_op jit(solution)/shard_map/ppermute | solution.py:826
  305.4 10.1 %collective-permute-start.6 = (bf16[48,512]{1,0:T(8,128)(2,1)S(1)}, bf16[48,512]{1,0:T(8,128)(2,1)S(1)}, u32[]{:S(2)}, u32[]{:S(2)}) collective-permute-start(bf16[48,512]{1,0:T(8,128)(2,1)S(1)} %get-tuple-element.158), channel_id=1, source_target_pairs={{0,16},{2,18},{4,20},{6,22},{8,24},{10,26},{12,28},{14,30},{16,0},... | collective-permute-start | bytes 147464 | tf_op jit(solution)/shard_map/ppermute | solution.py:826
  305.4 11.9 %collective-permute-start.7 = (bf16[48,512]{1,0:T(8,128)(2,1)S(1)}, bf16[48,512]{1,0:T(8,128)(2,1)S(1)}, u32[]{:S(2)}, u32[]{:S(2)}) collective-permute-start(bf16[48,512]{1,0:T(8,128)(2,1)S(1)} %get-tuple-element.157), channel_id=1, source_target_pairs={{0,24},{2,26},{4,28},{6,30},{8,0},{10,2},{12,4},{14,6},{16,8},{18,... | collective-permute-start | bytes 147464 | tf_op jit(solution)/shard_map/ppermute | solution.py:826
  310.5 28.9 %collective-permute-start.19 = (bf16[4,2,48,1664]{3,2,0,1:T(8,128)(2,1)S(1)}, bf16[4,2,48,1664]{3,2,0,1:T(8,128)(2,1)S(1)}, u32[]{:S(2)}, u32[]{:S(2)}) collective-permute-start(bf16[4,2,48,1664]{3,2,0,1:T(8,128)(2,1)S(1)} %fusion.1), channel_id=1, source_target_pairs={{0,4},{2,6},{4,0},{6,2},{8,12},{10,14},{12,8},{14,10},{16,20},{18,... | collective-permute-start | bytes 3833864 | tf_op jit(solution)/shard_map/ppermute | solution.py:821
  314.4 33.2 %collective-permute-start.14 = (bf16[4,2,48,1792]{3,2,0,1:T(8,128)(2,1)S(1)}, bf16[4,2,48,1792]{3,2,0,1:T(8,128)(2,1)S(1)}, u32[]{:S(2)}, u32[]{:S(2)}) collective-permute-start(bf16[4,2,48,1792]{3,2,0,1:T(8,128)(2,1)S(1)} %fusion), channel_id=1, source_target_pairs={{0,2},{2,0},{4,6},{6,4},{8,10},{10,8},{12,14},{14,12},{16,18},{18,... | collective-permute-start | bytes 4128776 | tf_op jit(solution)/shard_map/ppermute | solution.py:821
  321.0 83.9 %collective-permute-start.1 = (f32[1024,768]{1,0:T(8,128)S(1)}, f32[1024,768]{1,0:T(8,128)}, u32[]{:S(2)}, u32[]{:S(2)}) collective-permute-start(f32[1024,768]{1,0:T(8,128)S(1)} %copy-done.5), channel_id=1, source_target_pairs={{0,1},{1,0},{2,3},{3,2},{4,5},{5,4},{6,7},{7,6},{8,9},{9,8},{10,11... | collective-permute-start | bytes 9437192 | tf_op jit(solution)/shard_map/ppermute | solution.py:816
  322.0 73.6 %collective-permute-start = (bf16[1024,768]{1,0:T(8,128)(2,1)}, bf16[1024,768]{1,0:T(8,128)(2,1)}, u32[]{:S(2)}, u32[]{:S(2)}) collective-permute-start(bf16[1024,768]{1,0:T(8,128)(2,1)} %get-tuple-element.54), channel_id=1, source_target_pairs={{0,1},{1,0},{2,3},{3,2},{4,5},{5,4},{6,7},{7,6},{8,9},{9,8},{10,11... | collective-permute-start | bytes 4718600 | tf_op jit(solution)/shard_map/ppermute | solution.py:816
  339.7 19.1 %collective-permute-start.20 = (bf16[4,48,1664]{2,1,0:T(8,128)(2,1)S(1)}, bf16[4,48,1664]{2,1,0:T(8,128)(2,1)S(1)}, u32[]{:S(2)}, u32[]{:S(2)}) collective-permute-start(bf16[4,48,1664]{2,1,0:T(8,128)(2,1)S(1)} %fusion.3), channel_id=1, source_target_pairs={{0,2},{2,0},{4,6},{6,4},{8,10},{10,8},{12,14},{14,12},{16,18},{18,... | collective-permute-start | bytes 1916936 | tf_op jit(solution)/shard_map/ppermute | solution.py:821
  348.0 13.3 %collective-permute-start.15 = (bf16[4,48,1792]{2,1,0:T(8,128)(2,1)S(1)}, bf16[4,48,1792]{2,1,0:T(8,128)(2,1)S(1)}, u32[]{:S(2)}, u32[]{:S(2)}) collective-permute-start(bf16[4,48,1792]{2,1,0:T(8,128)(2,1)S(1)} %fusion.2), channel_id=1, source_target_pairs={{0,4},{2,6},{4,0},{6,2},{8,12},{10,14},{12,8},{14,10},{16,20},{18,... | collective-permute-start | bytes 2064392 | tf_op jit(solution)/shard_map/ppermute | solution.py:821
  359.0 9.0 %collective-permute-start.21 = (bf16[48,1664]{1,0:T(8,128)(2,1)S(1)}, bf16[48,1664]{1,0:T(8,128)(2,1)S(1)}, u32[]{:S(2)}, u32[]{:S(2)}) collective-permute-start(bf16[48,1664]{1,0:T(8,128)(2,1)S(1)} %get-tuple-element.148), channel_id=1, source_target_pairs={{0,8},{2,10},{4,12},{6,14},{8,16},{10,18},{12,20},{14,22},{16,24},... | collective-permute-start | bytes 479240 | tf_op jit(solution)/shard_map/ppermute | solution.py:826
  359.1 18.0 %collective-permute-start.22 = (bf16[48,1664]{1,0:T(8,128)(2,1)S(1)}, bf16[48,1664]{1,0:T(8,128)(2,1)S(1)}, u32[]{:S(2)}, u32[]{:S(2)}) collective-permute-start(bf16[48,1664]{1,0:T(8,128)(2,1)S(1)} %get-tuple-element.150), channel_id=1, source_target_pairs={{0,16},{2,18},{4,20},{6,22},{8,24},{10,26},{12,28},{14,30},{16,0},... | collective-permute-start | bytes 479240 | tf_op jit(solution)/shard_map/ppermute | solution.py:826
  361.3 15.8 %collective-permute-start.23 = (bf16[48,1664]{1,0:T(8,128)(2,1)S(1)}, bf16[48,1664]{1,0:T(8,128)(2,1)S(1)}, u32[]{:S(2)}, u32[]{:S(2)}) collective-permute-start(bf16[48,1664]{1,0:T(8,128)(2,1)S(1)} %get-tuple-element.149), channel_id=1, source_target_pairs={{0,24},{2,26},{4,28},{6,30},{8,0},{10,2},{12,4},{14,6},{16,8},{18,... | collective-permute-start | bytes 479240 | tf_op jit(solution)/shard_map/ppermute | solution.py:826
  368.0 13.0 %collective-permute-start.16 = (bf16[48,1792]{1,0:T(8,128)(2,1)S(1)}, bf16[48,1792]{1,0:T(8,128)(2,1)S(1)}, u32[]{:S(2)}, u32[]{:S(2)}) collective-permute-start(bf16[48,1792]{1,0:T(8,128)(2,1)S(1)} %get-tuple-element.145), channel_id=1, source_target_pairs={{0,8},{2,10},{4,12},{6,14},{8,16},{10,18},{12,20},{14,22},{16,24},... | collective-permute-start | bytes 516104 | tf_op jit(solution)/shard_map/ppermute | solution.py:826
  377.1 10.0 %collective-permute-start.17 = (bf16[48,1792]{1,0:T(8,128)(2,1)S(1)}, bf16[48,1792]{1,0:T(8,128)(2,1)S(1)}, u32[]{:S(2)}, u32[]{:S(2)}) collective-permute-start(bf16[48,1792]{1,0:T(8,128)(2,1)S(1)} %get-tuple-element.147), channel_id=1, source_target_pairs={{0,16},{2,18},{4,20},{6,22},{8,24},{10,26},{12,28},{14,30},{16,0},... | collective-permute-start | bytes 516104 | tf_op jit(solution)/shard_map/ppermute | solution.py:826
  377.1 10.0 %collective-permute-start.18 = (bf16[48,1792]{1,0:T(8,128)(2,1)S(1)}, bf16[48,1792]{1,0:T(8,128)(2,1)S(1)}, u32[]{:S(2)}, u32[]{:S(2)}) collective-permute-start(bf16[48,1792]{1,0:T(8,128)(2,1)S(1)} %get-tuple-element.146), channel_id=1, source_target_pairs={{0,24},{2,26},{4,28},{6,30},{8,0},{10,2},{12,4},{14,6},{16,8},{18,... | collective-permute-start | bytes 516104 | tf_op jit(solution)/shard_map/ppermute | solution.py:826
  (50 other events, 269.9 us)
